TPU v7x, 32 devices: a whole 2x2x4 slice. The times are simulated.
32 devices in a mesh: wide: 8 (over y, x, core), narrow: 4 (over z).
Axes of the slice: x: 2, y: 2, z: 4, core: 2. Of those that a mesh axis runs over, the one named last changes fastest.
Arguments:
- inputs: bfloat16 [8, 2048, 1120], P('wide', 'narrow'), may hold values from -6 to 6
- cell_lengths: int32 [8, 32], P('wide'), may hold values from 1 to 512, 2048 in all within a row
- w_qkv: bfloat16 [1120, 3360], P('narrow'), may hold values from -0.1875 to 0.1875
- w_out: bfloat16 [1120, 1120], P('narrow'), may hold values from -0.5 to 0.5
- w_fc: bfloat16 [1120, 4480], P('narrow'), may hold values from -0.1875 to 0.1875
- w_proj: bfloat16 [4480, 1120], P('narrow'), may hold values from -0.09375 to 0.09375
- b_query: bfloat16 [1120], P('narrow'), may hold values from -3 to 3
- b_value: bfloat16 [1120], P('narrow'), may hold values from -3 to 3
- b_out: bfloat16 [1120], P('narrow'), may hold values from -3 to 3
- b_fc: bfloat16 [4480], P('narrow'), may hold values from -3 to 3
- b_proj: bfloat16 [1120], P('narrow'), may hold values from -3 to 3
- gain_attn: bfloat16 [1120], P('narrow'), may hold values from 0.25 to 1.75
- shift_attn: bfloat16 [1120], P('narrow'), may hold values from -3 to 3
- gain_mlp: bfloat16 [1120], P('narrow'), may hold values from 0.25 to 1.75
- shift_mlp: bfloat16 [1120], P('narrow'), may hold values from -3 to 3
- cotangent: bfloat16 [8, 2048, 1120], P('wide', 'narrow'), may hold values from -6 to 6
Outputs:
- outputs: bfloat16 [8, 2048, 1120], P('wide', 'narrow')
- d_inputs: float32 [8, 2048, 1120], P('wide', 'narrow')
- grad_wqkv: float32 [1120, 3360], P('narrow')
- grad_wout: float32 [1120, 1120], P('narrow')
- grad_wfc: float32 [1120, 4480], P('narrow')
- grad_wproj: float32 [4480, 1120], P('narrow')
- grad_bquery: float32 [1120], P('narrow')
- grad_bvalue: float32 [1120], P('narrow')
- grad_bout: float32 [1120], P('narrow')
- grad_bfc: float32 [4480], P('narrow')
- grad_bproj: float32 [1120], P('narrow')
- grad_gattn: float32 [1120], P('narrow')
- grad_sattn: float32 [1120], P('narrow')
- grad_gmlp: float32 [1120], P('narrow')
- grad_smlp: float32 [1120], P('narrow')
Inputs may be any that keep to these rules, and one draw needn't show every extreme that they name: `cell_lengths`: each row's 32 cell lengths sum to 2048; every row's longest cell has exactly 512 positions.
All inputs are finite; a program needn't handle non-finite values.
Results may differ from a plain program's by a relative error of at most 0.012.
The roundings to bfloat16 on the way count: a program that leaves them out, or rounds other values in their place, can miss the bound.
Values may be sent and summed in bfloat16 or wider, within the bound.
No kernel may reach another device: no remote copies, remote signals or barrier semaphores. Data moves between devices by JAX's collectives and lax.ppermute only.
A program may use at most 320 MiB of HBM per device.

v0:
```python
import jax
import jax.numpy as jnp
from jax import lax
from jax.sharding import PartitionSpec as P

HEADS = 20
HEAD = 56


EPS = 1e-05


def from_behind(block, axis, distance):
    devices = range(lax.axis_size(axis))
    route = [(i - distance, i) for i in devices if i - distance in devices]
    return lax.ppermute(block, axis, route)


def layernorm_forward_pass(values, norm_gain, norm_shift):
    row_mean = jnp.mean(values, axis=-1, keepdims=True)
    centered = values - row_mean
    row_var = jnp.mean(centered * centered, axis=-1, keepdims=True)
    inv_std = lax.rsqrt(row_var + EPS)
    normed = centered * inv_std
    return (normed * norm_gain + norm_shift, normed, inv_std)


def layernorm_backward_pass(incoming, normed, inv_std, norm_gain):
    grad_gain = jnp.sum(incoming * normed, axis=0)
    grad_shift = jnp.sum(incoming, axis=0)
    scaled_grad = incoming * norm_gain
    mean_grad = jnp.mean(scaled_grad, axis=-1, keepdims=True)
    mean_proj = jnp.mean(scaled_grad * normed, axis=-1, keepdims=True)
    return (inv_std * (scaled_grad - mean_grad - normed * mean_proj), grad_gain, grad_shift)


def exact_gelu(values):
    return jax.nn.gelu(values, approximate=False)


def masked_scores(queries, key_win, allowed, score_scale):
    scores = (
        jnp.einsum("qhd,khd->hqk", queries, key_win, preferred_element_type=jnp.float32)
        * score_scale
    )
    return jnp.where(allowed, scores, -1e30)


def shards(
    inputs,
    cell_lengths,
    w_qkv,
    w_out,
    w_fc,
    w_proj,
    b_query,
    b_value,
    b_out,
    b_fc,
    b_proj,
    gain_attn,
    shift_attn,
    gain_mlp,
    shift_mlp,
    cotangent,
):
    rows_dev, span_len, model_width = inputs.shape
    tokens = rows_dev * span_len
    narrow_count = lax.axis_size("narrow")
    wide_count = lax.axis_size("wide")
    score_scale = HEAD ** (-0.5)
    gathered = (
        lax.all_gather(w_qkv, "narrow", axis=0, tiled=True),
        lax.all_gather(w_out, "narrow", axis=0, tiled=True),
        lax.all_gather(w_fc, "narrow", axis=0, tiled=True),
        lax.all_gather(w_proj, "narrow", axis=0, tiled=True),
        lax.all_gather(b_query, "narrow", axis=0, tiled=True),
        lax.all_gather(b_value, "narrow", axis=0, tiled=True),
        lax.all_gather(b_out, "narrow", axis=0, tiled=True),
        lax.all_gather(b_fc, "narrow", axis=0, tiled=True),
        lax.all_gather(b_proj, "narrow", axis=0, tiled=True),
        lax.all_gather(gain_attn, "narrow", axis=0, tiled=True),
        lax.all_gather(shift_attn, "narrow", axis=0, tiled=True),
        lax.all_gather(gain_mlp, "narrow", axis=0, tiled=True),
        lax.all_gather(shift_mlp, "narrow", axis=0, tiled=True),
    )
    mat_qkv, mat_out, mat_fc, mat_proj = (gathered[0], gathered[1], gathered[2], gathered[3])
    vectors = [v.astype(jnp.float32) for v in gathered[4:]]
    (
        bias_query,
        bias_value,
        bias_out,
        bias_fc,
        bias_proj,
        first_norm_gain,
        first_norm_shift,
        second_norm_gain,
        second_norm_shift,
    ) = vectors
    span_index = lax.axis_index("narrow")
    starts = jnp.cumsum(cell_lengths, axis=-1) - cell_lengths
    window_pos = (span_index - 1) * span_len + jnp.arange(2 * span_len, dtype=jnp.int32)
    cell_ids = (
        jnp.sum((starts[:, None, :] <= window_pos[None, :, None]).astype(jnp.int32), axis=-1) - 1
    )
    query_ids = cell_ids[:, span_len:]
    causal = jnp.arange(2 * span_len)[None, :] <= jnp.arange(span_len)[:, None] + span_len
    allowed = ((query_ids[:, :, None] == cell_ids[:, None, :]) & causal[None])[:, None]
    residual_stream = inputs.astype(jnp.float32).reshape(tokens, model_width)
    normalized_layer_input, first_standardized, first_inverse_deviation = layernorm_forward_pass(
        residual_stream, first_norm_gain, first_norm_shift
    )
    attn_in = normalized_layer_input.astype(jnp.bfloat16)
    projected = jnp.dot(attn_in, mat_qkv, preferred_element_type=jnp.float32)
    queries = (projected[:, :model_width] + bias_query).astype(jnp.bfloat16)
    queries = queries.reshape(rows_dev, span_len, HEADS, HEAD)
    kv_bias = jnp.concatenate([jnp.zeros_like(bias_value), bias_value])
    kv_own = (
        (projected[:, model_width:] + kv_bias)
        .astype(jnp.bfloat16)
        .reshape(rows_dev, span_len, 2 * model_width)
    )
    kv_prev = from_behind(kv_own, "narrow", 1)
    kv_win = jnp.concatenate([kv_prev, kv_own], axis=1)
    key_win = kv_win[..., :model_width].reshape(rows_dev, 2 * span_len, HEADS, HEAD)
    val_win = kv_win[..., model_width:].reshape(rows_dev, 2 * span_len, HEADS, HEAD)

    def attend_row(item):
        row_q, row_k, row_v, row_allowed = item
        masked = masked_scores(row_q, row_k, row_allowed, score_scale)
        row_max = jnp.max(masked, axis=-1, keepdims=True)
        exponent = jnp.exp(masked - row_max)
        row_total = jnp.sum(exponent, axis=-1, keepdims=True)
        row_probs = (exponent / row_total).astype(jnp.bfloat16)
        row_log = row_max + jnp.log(row_total)
        row_mixed = jnp.einsum("hqk,khd->qhd", row_probs, row_v, preferred_element_type=jnp.float32)
        return (row_mixed, row_probs, row_log)

    attn_mixed, attn_probs, log_total = lax.map(attend_row, (queries, key_win, val_win, allowed))
    attn_mixed = attn_mixed.reshape(tokens, model_width).astype(jnp.bfloat16)
    post_attention_state = residual_stream + (
        jnp.dot(attn_mixed, mat_out, preferred_element_type=jnp.float32) + bias_out
    )
    normalized_middle_state, second_standardized, second_inverse_deviation = layernorm_forward_pass(
        post_attention_state, second_norm_gain, second_norm_shift
    )
    mlp_in = normalized_middle_state.astype(jnp.bfloat16)
    pre_act = jnp.dot(mlp_in, mat_fc, preferred_element_type=jnp.float32) + bias_fc
    hidden = exact_gelu(pre_act).astype(jnp.bfloat16)
    result = post_attention_state + (
        jnp.dot(hidden, mat_proj, preferred_element_type=jnp.float32) + bias_proj
    )
    outputs = result.astype(jnp.bfloat16).reshape(rows_dev, span_len, model_width)
    regathered = (
        lax.all_gather(w_qkv, "narrow", axis=0, tiled=True),
        lax.all_gather(w_out, "narrow", axis=0, tiled=True),
        lax.all_gather(w_fc, "narrow", axis=0, tiled=True),
        lax.all_gather(w_proj, "narrow", axis=0, tiled=True),
        lax.all_gather(gain_attn, "narrow", axis=0, tiled=True),
        lax.all_gather(gain_mlp, "narrow", axis=0, tiled=True),
    )
    back_qkv, back_out, back_fc, back_proj = (
        regathered[0],
        regathered[1],
        regathered[2],
        regathered[3],
    )
    first_gain_pullback = regathered[4].astype(jnp.float32)
    second_gain_pullback = regathered[5].astype(jnp.float32)
    grad_branch = cotangent.reshape(tokens, model_width)
    grad_out = grad_branch.astype(jnp.float32)
    grad_wproj = jnp.einsum("tf,td->fd", hidden, grad_branch, preferred_element_type=jnp.float32)
    grad_bproj = jnp.sum(grad_out, axis=0)
    grad_hidden = jnp.einsum(
        "td,fd->tf", grad_branch, back_proj, preferred_element_type=jnp.float32
    )
    gelu_value, gelu_back = jax.vjp(exact_gelu, pre_act)
    grad_pre = gelu_back(grad_hidden)[0].astype(jnp.bfloat16)
    grad_wfc = jnp.einsum("td,tf->df", mlp_in, grad_pre, preferred_element_type=jnp.float32)
    grad_bfc = jnp.sum(grad_pre.astype(jnp.float32), axis=0)
    middle_state_gradient = jnp.einsum(
        "tf,df->td", grad_pre, back_fc, preferred_element_type=jnp.float32
    )
    post_attention_gradient, second_gain_gradient, second_shift_gradient = layernorm_backward_pass(
        middle_state_gradient, second_standardized, second_inverse_deviation, second_gain_pullback
    )
    post_attention_gradient = post_attention_gradient + grad_out
    grad_attn = post_attention_gradient.astype(jnp.bfloat16)
    grad_wout = jnp.einsum("td,te->de", attn_mixed, grad_attn, preferred_element_type=jnp.float32)
    grad_bout = jnp.sum(grad_attn.astype(jnp.float32), axis=0)
    grad_mixed = jnp.einsum("te,de->td", grad_attn, back_out, preferred_element_type=jnp.float32)
    grad_mixed = grad_mixed.astype(jnp.bfloat16).reshape(rows_dev, span_len, HEADS, HEAD)

    def attend_back(item):
        row_q, row_k, row_v, row_allowed, row_log, row_probs, row_grad = item
        masked_again = masked_scores(row_q, row_k, row_allowed, score_scale)
        soft_again = jnp.exp(masked_again - row_log)
        grad_probs = jnp.einsum("qhd,khd->hqk", row_grad, row_v, preferred_element_type=jnp.float32)
        grad_val = jnp.einsum(
            "hqk,qhd->khd", row_probs, row_grad, preferred_element_type=jnp.float32
        )
        row_dot = jnp.sum(grad_probs * soft_again, axis=-1, keepdims=True)
        grad_scores = (soft_again * (grad_probs - row_dot)).astype(jnp.bfloat16)
        grad_query = (
            jnp.einsum("hqk,khd->qhd", grad_scores, row_k, preferred_element_type=jnp.float32)
            * score_scale
        )
        grad_key = (
            jnp.einsum("hqk,qhd->khd", grad_scores, row_q, preferred_element_type=jnp.float32)
            * score_scale
        )
        return (grad_query, grad_key, grad_val)

    grad_query, grad_key, grad_val = lax.map(
        attend_back, (queries, key_win, val_win, allowed, log_total, attn_probs, grad_mixed)
    )
    grad_kv = jnp.concatenate(
        [
            grad_key.reshape(rows_dev, 2 * span_len, model_width),
            grad_val.reshape(rows_dev, 2 * span_len, model_width),
        ],
        axis=-1,
    )
    from_next = from_behind(grad_kv[:, :span_len].astype(jnp.bfloat16), "narrow", -1).astype(
        jnp.float32
    )
    grad_kv_own = (
        (grad_kv[:, span_len:] + from_next).astype(jnp.bfloat16).reshape(tokens, 2 * model_width)
    )
    grad_qrows = grad_query.astype(jnp.bfloat16).reshape(tokens, model_width)
    grad_projected = jnp.concatenate([grad_qrows, grad_kv_own], axis=-1)
    grad_wqkv = jnp.einsum("td,te->de", attn_in, grad_projected, preferred_element_type=jnp.float32)
    grad_bquery = jnp.sum(grad_qrows.astype(jnp.float32), axis=0)
    grad_bvalue = jnp.sum(grad_kv_own[:, model_width:].astype(jnp.float32), axis=0)
    normalized_gradient = jnp.einsum(
        "te,de->td", grad_projected, back_qkv, preferred_element_type=jnp.float32
    )
    layer_input_gradient, first_gain_gradient, first_shift_gradient = layernorm_backward_pass(
        normalized_gradient, first_standardized, first_inverse_deviation, first_gain_pullback
    )
    d_inputs = (layer_input_gradient + post_attention_gradient).reshape(
        rows_dev, span_len, model_width
    )
    vector_grads = [
        grad_bquery,
        grad_bvalue,
        grad_bout,
        grad_bfc,
        grad_bproj,
        first_gain_gradient,
        first_shift_gradient,
        second_gain_gradient,
        second_shift_gradient,
    ]
    packed = jnp.concatenate([v.reshape(narrow_count, -1) for v in vector_grads], axis=1)

    def spread(incoming):
        flattened = incoming.reshape(narrow_count, wide_count, -1)
        return jnp.swapaxes(flattened, 0, 1).reshape(wide_count * narrow_count, -1)

    reduced = (
        lax.psum_scatter(spread(grad_wqkv), ("wide", "narrow"), scatter_dimension=0, tiled=True),
        lax.psum_scatter(spread(grad_wout), ("wide", "narrow"), scatter_dimension=0, tiled=True),
        lax.psum_scatter(spread(grad_wfc), ("wide", "narrow"), scatter_dimension=0, tiled=True),
        lax.psum_scatter(spread(grad_wproj), ("wide", "narrow"), scatter_dimension=0, tiled=True),
        lax.psum_scatter(spread(packed), ("wide", "narrow"), scatter_dimension=0, tiled=True),
    )
    reduced = (
        lax.all_gather(reduced[0].astype(jnp.bfloat16), "wide", axis=0, tiled=True).astype(
            jnp.float32
        ),
        lax.all_gather(reduced[1].astype(jnp.bfloat16), "wide", axis=0, tiled=True).astype(
            jnp.float32
        ),
        lax.all_gather(reduced[2].astype(jnp.bfloat16), "wide", axis=0, tiled=True).astype(
            jnp.float32
        ),
        lax.all_gather(reduced[3].astype(jnp.bfloat16), "wide", axis=0, tiled=True).astype(
            jnp.float32
        ),
        lax.all_gather(reduced[4].astype(jnp.bfloat16), "wide", axis=0, tiled=True).astype(
            jnp.float32
        ),
    )
    shard_qkv = reduced[0].reshape(w_qkv.shape)
    shard_out = reduced[1].reshape(w_out.shape)
    shard_fc = reduced[2].reshape(w_fc.shape)
    shard_proj = reduced[3].reshape(w_proj.shape)
    packed_shard = reduced[4].reshape(-1)
    shard_width = b_query.shape[0]
    shard_hidden = b_fc.shape[0]
    lengths_list = [
        shard_width,
        shard_width,
        shard_width,
        shard_hidden,
        shard_width,
        shard_width,
        shard_width,
        shard_width,
        shard_width,
    ]
    offsets = [0]
    for piece_len in lengths_list:
        offsets.append(offsets[-1] + piece_len)
    pieces = [packed_shard[offsets[i] : offsets[i + 1]] for i in range(len(lengths_list))]
    return (
        outputs,
        d_inputs,
        shard_qkv,
        shard_out,
        shard_fc,
        shard_proj,
        pieces[0],
        pieces[1],
        pieces[2],
        pieces[3],
        pieces[4],
        pieces[5],
        pieces[6],
        pieces[7],
        pieces[8],
    )


def solution(mesh):
    in_specs = (
        P("wide", "narrow", None),
        P("wide", None),
        P("narrow", None),
        P("narrow", None),
        P("narrow", None),
        P("narrow", None),
        P("narrow"),
        P("narrow"),
        P("narrow"),
        P("narrow"),
        P("narrow"),
        P("narrow"),
        P("narrow"),
        P("narrow"),
        P("narrow"),
        P("wide", "narrow", None),
    )
    out_specs = (
        P("wide", "narrow", None),
        P("wide", "narrow", None),
        P("narrow", None),
        P("narrow", None),
        P("narrow", None),
        P("narrow", None),
        P("narrow"),
        P("narrow"),
        P("narrow"),
        P("narrow"),
        P("narrow"),
        P("narrow"),
        P("narrow"),
        P("narrow"),
        P("narrow"),
    )
    return jax.shard_map(shards, mesh=mesh, in_specs=in_specs, out_specs=out_specs, check_vma=False)
```

profile of v0, /device:TPU:0, one launch (start us, length us, event | category | flops | bytes accessed | tf_op | source)
XLA Modules:
  0.0 2124.8 jit_solution(16221992524066549971)
XLA Ops:
  13.8 26.3 %all-reduce.16 = (bf16[1120]{0:T(1024)(128)(2,1)S(1)}, bf16[1120]{0:T(1024)(128)(2,1)S(1)}, bf16[1120]{0:T(1024)(128)(2,1)S(1)}, bf16[1120]{0:T(1024)(128)(2,1)S...) all-reduce(bf16[1120]{0:T(1024)(128)(2,1)S(1)} %dynamic-update-slic, ...), channel_id=1, replica_groups=mesh['wide'=8,'narrow'=4] {'narrow'}, use_global_device_ids=true, to_apply=%add.2 | all-reduce | flops 13440 | bytes 53760
  40.9 111.3 %all-gather.13.cloned.1.call-done = bf16[1120,3360]{1,0:T(8,128)(2,1)} async-done(((bf16[280,3360]{1,0:T(8,128)(2,1)}), bf16[1120,3360]{1,0:T(8,128)(2,1)}) %all-gather.13.cloned.1.call-update) | async-done | bytes 7526416 | tf_op jit(solution)/shard_map/all_gather | solution.py:73
  170.2 81.0 %collective-permute-done = bf16[1,512,2240]{1,2,0:T(8,128)(2,1)} collective-permute-done((bf16[1,512,2240]{1,2,0:T(8,128)(2,1)S(1)}, bf16[1,512,2240]{1,2,0:T(8,128)(2,1)}, u32[]{:S(2)}, u32[]{:S(2)}) %collective-permute-start) | collective-permute-done | bytes 2293792 | tf_op jit(solution)/shard_map/ppermute | solution.py:16
  255.9 19.9 fusion.1
  275.8 19.1 fusion
  294.9 26.0 %divide_convert_fusion = bf16[20,512,1024]{2,1,0:T(8,128)(2,1)} fusion(f32[20,512,1024]{2,1,0:T(8,128)} %get-tuple-element.110, f32[20,512]{1,0:T(8,128)S(1)} %fusion, f32[20,512]{1,0:T(8,128)S(1)} %get-tuple-element.109, pred[512,1024]{1,0:T(8,128)(4,1)S(1)} %fusion.39), kind=kLoop, calls=%fused_computation.3 | loop fusion | flops 52428800 | bytes 63520768 | tf_op jit(solution)/shard_map/while/body/eval_jaxpr/convert_element_type | solution.py:134
  321.0 11.6 convolution_convert_fusion.1
  337.1 81.4 %all-gather.17.cloned.1.call-done = bf16[1120,4480]{1,0:T(8,128)(2,1)} async-done(((bf16[280,4480]{1,0:T(8,128)(2,1)}), bf16[1120,4480]{1,0:T(8,128)(2,1)}) %all-gather.17.cloned.1.call-update) | async-done | bytes 10035216 | tf_op jit(solution)/shard_map/all_gather | solution.py:75
  418.5 33.5 %multiply_convert_fusion.1 = (bf16[512,4480]{1,0:T(8,128)(2,1)}, f32[512,4480]{1,0:T(8,128)}, f32[512,4480]{1,0:T(8,128)}) fusion(f32[4480]{0:T(1024)S(1)} %convert_element_type.152, bf16[1120,4480]{1,0:T(8,128)(2,1)} %all-gather.17.cloned.1.call-done, f32[512,1120]{0,1:T(8,128)S(1)} %get-tuple-element.112, f32[1120]{0:T(1024)S(1)} %convert_element_type.150, ...), kind=kOutput, calls=%fused_computation.16 | convolution fusion | flops 5292277760 | bytes 35297536 | tf_op jit(solution)/shard_map/dot_general | solution.py:148
  452.0 147.4 %all-gather.19.cloned.1.call-done = bf16[4480,1120]{1,0:T(8,128)(2,1)} async-done(((bf16[1120,1120]{1,0:T(8,128)(2,1)}), bf16[4480,1120]{1,0:T(8,128)(2,1)}) %all-gather.19.cloned.1.call-update) | async-done | bytes 10035216 | tf_op jit(solution)/shard_map/all_gather | solution.py:76
  599.4 16.8 convert_reduce_fusion
  640.6 32.3 %multiply_reduce_fusion = (f32[20,512]{1,0:T(8,128)S(1)}, f32[20,512,1024]{2,1,0:T(8,128)}) fusion(f32[20,512,1024]{2,1,0:T(8,128)} %get-tuple-element.110, f32[20,512]{1,0:T(8,128)S(1)} %log_add_fusion, pred[512,1024]{1,0:T(8,128)(4,1)S(1)} %fusion.39, bf16[512,20,56]{0,2,1:T(8,128)(2,1)} %bitcast.149, bf16[1024,20,56]{0,2,1:T(8,128)(2,1)} %bitcast.141), kind=kOutput, calls=%fused_computation.1 | convolution fusion | flops 1226823680 | bytes 87932928 | tf_op jit(solution)/shard_map/while/body/eval_jaxpr/qhd,khd->hqk/dot_general | solution.py:198
  673.0 34.0 %multiply_convert_fusion = bf16[20,512,1024]{2,1,0:T(8,128)(2,1)} fusion(f32[20,512,1024]{2,1,0:T(8,128)} %get-tuple-element.116, f32[20,512,1024]{2,1,0:T(8,128)} %get-tuple-element.110, f32[20,512]{1,0:T(8,128)S(1)} %get-tuple-element.115, f32[20,512]{1,0:T(8,128)S(1)} %log_add_fusion, pred[512,1024]{1,0:T(8,128)(4,1)S(1)} %fusion.39), kind=kLoop, calls=%fused_computation | loop fusion | flops 62914560 | bytes 105463808 | tf_op jit(solution)/shard_map/while/body/eval_jaxpr/convert_element_type | solution.py:203
  716.0 13.9 convert_reduce_fusion.8
  735.8 12.3 fusion.59
  770.2 24.2 %reshape.380 = f32[4,8,156800]{2,1,0:T(8,128)} reshape(f32[1120,4480]{1,0:T(8,128)} %fusion.59) | data formatting | bytes 40140800 | tf_op jit(solution)/shard_map/reshape | solution.py:258
  794.4 20.5 copy.58
  814.9 25.5 %reshape.381 = f32[32,156800]{1,0:T(8,128)} reshape(f32[8,4,156800]{2,1,0:T(4,128)} %bitcast.130) | data formatting | bytes 40140800 | tf_op jit(solution)/shard_map/reshape | solution.py:259
  840.3 13.3 fusion.40
  853.6 34.3 %reshape.384 = f32[4,8,156800]{2,1,0:T(8,128)} reshape(f32[4480,1120]{1,0:T(8,128)} %fusion.40) | data formatting | bytes 40140800 | tf_op jit(solution)/shard_map/reshape | solution.py:258
  888.0 20.5 copy.52
  908.5 25.7 %reshape.385 = f32[32,156800]{1,0:T(8,128)} reshape(f32[8,4,156800]{2,1,0:T(4,128)} %copy.52) | data formatting | bytes 40140800 | tf_op jit(solution)/shard_map/reshape | solution.py:259
  934.7 14.3 fusion.17
  961.2 17.0 reshape.372
  978.2 19.0 copy.59
  997.2 12.8 reshape.373
  1020.9 946.5 %all-reduce.18 = (bf16[32,117600]{1,0:T(8,128)(2,1)}, bf16[32,39200]{1,0:T(8,128)(2,1)}, bf16[32,156800]{1,0:T(8,128)(2,1)}, bf16[32,156800]{1,0:T(8,128)(2,1)}, bf16[32,420]{1,0:T(8,128)(2,1)S(1)}) all-reduce(f32[32,117600]{1,0:T(8,128)} %reshape.373, ...), channel_id=2, replica_groups=mesh['wide'=8,'narrow'=4] {'wide','narrow'}, use_global_device_ids=true, to_apply=%region_13.14.clone | all-reduce | flops 15066240 | bytes 90397440
  1977.5 13.2 all-gather.1
  2012.6 29.4 %convert_reduce_fusion.3 = f32[8,117600]{1,0:T(8,128)} fusion(bf16[8,1,117600]{2,1,0:T(2,128)(2,1)} %all-gather.21.cloned.1.call-done), kind=kLoop, calls=%fused_computation.42 | loop fusion | flops 940800 | bytes 5644800 | tf_op jit(solution)/shard_map/reshape | solution.py:285
  2049.9 17.7 convert_reduce_fusion.2
  2073.5 18.5 all-gather.25.cloned.1.call-done
  2092.0 17.9 convert_reduce_fusion.1
  (219 shorter events, 171.1 us)
Async XLA Ops:
  7.3 33.0 %copy-start.6 = (bf16[1,512,1120]{1,2,0:T(8,128)(2,1)S(1)}, bf16[1,512,1120]{1,2,0:T(8,128)(2,1)}, u32[]{:S(2)}) copy-start(bf16[1,512,1120]{1,2,0:T(8,128)(2,1)} %param.16) | copy-start | bytes 3440644
  7.3 144.9 %all-gather.13.cloned.1.call-start = ((), (), s32[]{:S(2)}) async-start(), calls=%async_computation | async-start | bytes 9676800 | tf_op jit(solution)/shard_map/all_gather | solution.py:73
  8.0 324.5 %all-gather.15.cloned.1.call-start = ((), (), s32[]{:S(2)}) async-start(), calls=%async_computation.1 | async-start | bytes 3225600 | tf_op jit(solution)/shard_map/all_gather | solution.py:74
  8.8 409.7 %all-gather.17.cloned.1.call-start = ((), (), s32[]{:S(2)}) async-start(), calls=%async_computation.2 | async-start | bytes 12544000 | tf_op jit(solution)/shard_map/all_gather | solution.py:75
  9.5 589.8 %all-gather.19.cloned.1.call-start = ((), (), s32[]{:S(2)}) async-start(), calls=%async_computation.3 | async-start | bytes 12902400 | tf_op jit(solution)/shard_map/all_gather | solution.py:76
  40.2 119.6 %copy-start.25 = (f32[1120]{0:T(1024)}, f32[1120]{0:T(1024)S(1)}, u32[]{:S(2)}) copy-start(f32[1120]{0:T(1024)S(1)} %convert_element_type.138) | copy-start | bytes 13444
  40.2 112.0 %copy-start.18 = (f32[1120]{0:T(1024)}, f32[1120]{0:T(1024)S(1)}, u32[]{:S(2)}) copy-start(f32[1120]{0:T(1024)S(1)} %convert_element_type.137) | copy-start | bytes 13444
  40.5 111.7 %copy-start.21 = (f32[512]{0:T(512)}, f32[512]{0:T(512)S(1)}, u32[]{:S(2)}) copy-start(f32[512]{0:T(512)S(1)} %broadcast_multiply_fusion.6) | copy-start | bytes 6148
  40.9 118.9 %copy-start.28 = (f32[512]{0:T(512)}, f32[512]{0:T(512)S(1)}, u32[]{:S(2)}) copy-start(f32[512]{0:T(512)S(1)} %add_rsqrt_fusion.1) | copy-start | bytes 6148
  163.0 88.2 %collective-permute-start = (bf16[1,512,2240]{1,2,0:T(8,128)(2,1)S(1)}, bf16[1,512,2240]{1,2,0:T(8,128)(2,1)}, u32[]{:S(2)}, u32[]{:S(2)}) collective-permute-start(bf16[1,512,2240]{1,2,0:T(8,128)(2,1)S(1)} %fusion.34), channel_id=1, source_target_pairs={{0,1},{1,2},{2,3},{4,5},{5,6},{6,7},{8,9},{9,10},{10,11},{12,13},{... | collective-permute-start | bytes 6881288 | tf_op jit(solution)/shard_map/ppermute | solution.py:16
  165.6 1846.9 %all-gather.21.cloned.1.call-start = ((), (), s32[]{:S(2)}) async-start(), calls=%async_computation.4 | async-start | bytes 4234752 | tf_op jit(solution)/shard_map/all_gather | solution.py:269
  255.9 19.9 copy-start.1
  294.9 26.1 %copy-start.2 = (bf16[1,1024,1120]{1,2,0:T(8,128)(2,1)S(1)}, bf16[1,1024,1120]{1,2,0:T(8,128)(2,1)}, u32[]{:S(2)}) copy-start(bf16[1,1024,1120]{1,2,0:T(8,128)(2,1)} %get-tuple-element.99) | copy-start | bytes 6881284
  336.7 279.4 %copy-start.9 = (f32[512,1120]{0,1:T(8,128)}, f32[512,1120]{0,1:T(8,128)S(1)}, u32[]{:S(2)}) copy-start(f32[512,1120]{0,1:T(8,128)S(1)} %get-tuple-element.112) | copy-start | bytes 6881284
  616.1 17.9 slice-start
  616.1 17.9 slice-start.1
  716.0 32.1 %copy-start = (f32[20,56,1024]{2,1,0:T(8,128)}, f32[20,56,1024]{2,1,0:T(8,128)S(1)}, u32[]{:S(2)}) copy-start(f32[20,56,1024]{2,1,0:T(8,128)S(1)} %broadcast_multiply_fusion) | copy-start | bytes 13762564
  729.9 18.2 slice-start.5
  749.9 199.2 %collective-permute-start.1 = (bf16[1,512,2240]{1,2,0:T(8,128)(2,1)}, bf16[1,512,2240]{1,2,0:T(8,128)(2,1)}, u32[]{:S(2)}, u32[]{:S(2)}) collective-permute-start(bf16[1,512,2240]{1,2,0:T(8,128)(2,1)} %fusion.11), channel_id=1, source_target_pairs={{1,0},{2,1},{3,2},{5,4},{6,5},{7,6},{9,8},{10,9},{11,10},{13,12},{... | collective-permute-start | bytes 6881288 | tf_op jit(solution)/shard_map/ppermute | solution.py:16
  814.9 25.5 %copy-start.15 = (bf16[1,512,1120]{1,2,0:T(8,128)(2,1)S(1)}, bf16[1,512,1120]{1,2,0:T(8,128)(2,1)}, u32[]{:S(2)}) copy-start(bf16[1,512,1120]{1,2,0:T(8,128)(2,1)} %param.31) | copy-start | bytes 3440644
  908.5 25.8 %copy-start.17 = (f32[1120]{0:T(1024)S(1)}, f32[1120]{0:T(1024)}, u32[]{:S(2)}) copy-start(f32[1120]{0:T(1024)} %get-tuple-element.94) | copy-start | bytes 13444
  908.5 25.9 %copy-start.20 = (f32[4480]{0:T(1024)S(1)}, f32[4480]{0:T(1024)}, u32[]{:S(2)}) copy-start(f32[4480]{0:T(1024)} %get-tuple-element.120) | copy-start | bytes 53764
  908.5 26.0 %copy-start.16 = (f32[1120]{0:T(1024)S(1)}, f32[1120]{0:T(1024)}, u32[]{:S(2)}) copy-start(f32[1120]{0:T(1024)} %get-tuple-element.100) | copy-start | bytes 13444
  908.5 26.0 %copy-start.24 = (f32[1120]{0:T(1024)S(1)}, f32[1120]{0:T(1024)}, u32[]{:S(2)}) copy-start(f32[1120]{0:T(1024)} %get-tuple-element.61) | copy-start | bytes 13444
  908.5 26.1 %copy-start.23 = (f32[1120]{0:T(1024)S(1)}, f32[1120]{0:T(1024)}, u32[]{:S(2)}) copy-start(f32[1120]{0:T(1024)} %get-tuple-element.78) | copy-start | bytes 13444
  908.5 26.2 %copy-start.11 = (f32[512,1120]{0,1:T(8,128)S(1)}, f32[512,1120]{0,1:T(8,128)}, u32[]{:S(2)}) copy-start(f32[512,1120]{0,1:T(8,128)} %copy-done.9) | copy-start | bytes 6881284
  908.5 26.2 %copy-start.27 = (f32[1120]{0:T(1024)S(1)}, f32[1120]{0:T(1024)}, u32[]{:S(2)}) copy-start(f32[1120]{0:T(1024)} %convert_element_type.154) | copy-start | bytes 13444
  1970.2 79.7 %all-gather.23.cloned.1.call-start = ((), (), s32[]{:S(2)}) async-start(), calls=%async_computation.5 | async-start | bytes 5644800 | tf_op jit(solution)/shard_map/all_gather | solution.py:275
  1973.0 35.2 %copy-start.32 = (f32[512]{0:T(512)S(1)}, f32[512]{0:T(512)}, u32[]{:S(2)}) copy-start(f32[512]{0:T(512)} %get-tuple-element.64) | copy-start | bytes 6148
  1973.0 35.2 %copy-start.31 = (f32[512]{0:T(512)S(1)}, f32[512]{0:T(512)}, u32[]{:S(2)}) copy-start(f32[512]{0:T(512)} %get-tuple-element.76) | copy-start | bytes 6148
  1973.0 35.9 %copy-start.4 = (f32[512,1120]{0,1:T(8,128)S(1)}, f32[512,1120]{0,1:T(8,128)}, u32[]{:S(2)}) copy-start(f32[512,1120]{0,1:T(8,128)} %copy-done.3) | copy-start | bytes 6881284
  1973.0 119.0 %all-gather.25.cloned.1.call-start = ((), (), s32[]{:S(2)}) async-start(), calls=%async_computation.6 | async-start | bytes 5644800 | tf_op jit(solution)/shard_map/all_gather | solution.py:278
  (28 other events, 180.9 us)
Sparse Core Ops, SparseCore 0:
  9.7 142.4 all-gather.12
  153.8 85.5 all-gather.14
  240.9 177.4 all-gather.16
  419.9 179.4 all-gather.18
  1970.3 36.9 all-gather.20
  2009.6 40.1 all-gather.22
  2051.8 40.1 all-gather.24
where the time goes:
time: 2130 us; the launch traced here: 2120 us
  blocking collectives  995 us (47%)
  waiting for transfers between devices  443 us (21%)
  local copies, waits for them, and re-layouts  261 us (12%)
  matrix products  233 us (11%)
  other arithmetic  173 us (8%)
    unnamed x2, blocking collectives  973 us
    all_gather x1, waiting for transfers between devices, shards(): lax.all_gather(w_proj, 'narrow', axis=0, tiled=True)  147 us
    reshape x8, local copies, waits for them, and re-layouts, spread(): flattened = incoming.reshape(narrow_count, wide_count, -1)  128 us
    all_gather x1, waiting for transfers between devices, shards(): lax.all_gather(w_qkv, 'narrow', axis=0, tiled=True)  111 us
    all_gather x1, waiting for transfers between devices, shards(): lax.all_gather(w_fc, 'narrow', axis=0, tiled=True)  81.4 us
    ppermute x2, waiting for transfers between devices, from_behind(): return lax.ppermute(block, axis, route)  81 us
    reshape x5, local copies, waits for them, and re-layouts, spread(): return jnp.swapaxes(flattened, 0, 1).reshape(wide_count * narrow_count, -1)  69.9 us
  transfers between devices with their start and end apart: 9, of which 6 were waited for; matrix products, arithmetic and copies ran while one was open for 19% of the time, Pallas kernels for 0%

commit v1 on v0

v1 whole, which is shorter than its diff:
```python
import functools

import jax
import jax.numpy as jnp
from jax import lax
from jax.experimental import pallas as pl
from jax.experimental.pallas import tpu as pltpu
from jax.sharding import PartitionSpec as P

HEADS = 20
HEAD = 56
EPS = 1e-05
BF = jnp.bfloat16
F32 = jnp.float32
ROOT_HALF = 0.7071067811865476
INV_ROOT_2PI = 0.3989422804014327
VMEM_LIMIT = 60 * 1024 * 1024


def params(n):
    return pltpu.CompilerParams(
        dimension_semantics=("arbitrary",) * n, vmem_limit_bytes=VMEM_LIMIT
    )


def mm(a, b):
    return jnp.dot(a, b, preferred_element_type=F32)


def mm_nt(a, b):
    return lax.dot_general(a, b, (((1,), (1,)), ((), ())), preferred_element_type=F32)


def mm_tn(a, b):
    return lax.dot_general(a, b, (((0,), (0,)), ((), ())), preferred_element_type=F32)


def standardize(values):
    mean = jnp.mean(values, axis=-1, keepdims=True)
    centered = values - mean
    var = jnp.mean(centered * centered, axis=-1, keepdims=True)
    inv = lax.rsqrt(var + EPS)
    return centered * inv, inv


def norm_pullback(grad, normed, inv, gain):
    scaled = grad * gain
    mean_grad = jnp.mean(scaled, axis=-1, keepdims=True)
    mean_proj = jnp.mean(scaled * normed, axis=-1, keepdims=True)
    return inv * (scaled - mean_grad - normed * mean_proj)


def head_window(h, width):
    low, high = h * HEAD, (h + 1) * HEAD
    a = low // 128 * 128
    b = min(-(-high // 128) * 128, width)
    lane = lax.broadcasted_iota(jnp.int32, (1, b - a), 1) + a
    return a, b, (lane >= low) & (lane < high)


def qkv_kernel(xp_ref, xo_ref, wq_ref, wk_ref, wv_ref, vec_ref, q_ref, k_ref, v_ref, nt_ref):
    step = pl.program_id(0)
    half = pl.num_programs(0) // 2
    x = jnp.where(step < half, xp_ref[...].astype(F32), xo_ref[...].astype(F32))
    normed, _ = standardize(x)
    n = (normed * vec_ref[0:1, :] + vec_ref[1:2, :]).astype(BF)
    k_ref[...] = mm(n, wk_ref[...]).astype(BF)
    v_ref[...] = (mm(n, wv_ref[...]) + vec_ref[3:4, :]).astype(BF)

    @pl.when(step >= half)
    def _():
        q_ref[...] = (mm(n, wq_ref[...]) + vec_ref[2:3, :]).astype(BF)
        nt_ref[...] = n.T


def ln_qkv(x_prev, x_own, wa, vec, tb):
    t, d = x_own.shape
    nb = t // tb
    own = lambda i: (jnp.maximum(i - nb, 0), 0)
    weight = lambda s: pl.BlockSpec((None, d, d), lambda i: (s, 0, 0))
    return pl.pallas_call(
        qkv_kernel,
        grid=(2 * nb,),
        in_specs=[
            pl.BlockSpec((tb, d), lambda i: (jnp.minimum(i, nb - 1), 0)),
            pl.BlockSpec((tb, d), own),
            weight(0),
            weight(1),
            weight(2),
            pl.BlockSpec(vec.shape, lambda i: (0, 0)),
        ],
        out_specs=[
            pl.BlockSpec((tb, d), own),
            pl.BlockSpec((tb, d), lambda i: (i, 0)),
            pl.BlockSpec((tb, d), lambda i: (i, 0)),
            pl.BlockSpec((d, tb), lambda i: (0, jnp.maximum(i - nb, 0))),
        ],
        out_shape=[
            jax.ShapeDtypeStruct((t, d), BF),
            jax.ShapeDtypeStruct((2 * t, d), BF),
            jax.ShapeDtypeStruct((2 * t, d), BF),
            jax.ShapeDtypeStruct((d, t), BF),
        ],
        compiler_params=params(1),
        name="ln_qkv",
    )(x_prev, x_own, wa, wa, wa, vec)


def attend_kernel(q_ref, k_ref, v_ref, qid_ref, kid_ref, o_ref, acc_ref):
    block, width = q_ref.shape
    band = kid_ref.shape[-1]
    base = pl.multiple_of(pl.program_id(0) * block, block)
    row = lax.broadcasted_iota(jnp.int32, (block, band), 0)
    col = lax.broadcasted_iota(jnp.int32, (block, band), 1)
    allowed = (qid_ref[...] == kid_ref[...]) & (col <= row + (band - block))
    bias = jnp.where(allowed, 0.0, -1e30)
    acc_ref[...] = jnp.zeros_like(acc_ref)
    for h in range(HEADS):
        a, b, lanes = head_window(h, width)
        query = jnp.where(lanes, q_ref[:, a:b].astype(F32), 0.0).astype(BF)
        scores = mm_nt(query, k_ref[pl.ds(base, band), a:b]) * HEAD**-0.5 + bias
        e = jnp.exp(scores - jnp.max(scores, axis=-1, keepdims=True))
        probs = (e / jnp.sum(e, axis=-1, keepdims=True)).astype(BF)
        out = mm(probs, v_ref[pl.ds(base, band), a:b])
        acc_ref[:, a:b] += jnp.where(lanes, out, 0.0)
    o_ref[...] = acc_ref[...].astype(BF)


def attend(q, k, v, qid, kid, block):
    t, d = q.shape
    band = kid.shape[-1]
    whole = pl.BlockSpec((2 * t, d), lambda i: (0, 0))
    return pl.pallas_call(
        attend_kernel,
        grid=(t // block,),
        in_specs=[
            pl.BlockSpec((block, d), lambda i: (i, 0)),
            whole,
            whole,
            pl.BlockSpec((block, 1), lambda i: (i, 0)),
            pl.BlockSpec((None, 1, band), lambda i: (i, 0, 0)),
        ],
        out_specs=pl.BlockSpec((block, d), lambda i: (i, 0)),
        out_shape=jax.ShapeDtypeStruct((t, d), BF),
        scratch_shapes=[pltpu.VMEM((block, d), F32)],
        compiler_params=params(1),
        name="attend",
    )(q, k, v, qid, kid)


def attend_back_kernel(
    q_ref, k_ref, v_ref, g_ref, qid_ref, kid_ref, dq_ref, prev_ref, own_ref, acc_ref, dk_ref, dv_ref
):
    step = pl.program_id(0)
    block, width = q_ref.shape
    band = kid_ref.shape[0]
    span = dk_ref.shape[0] // 2
    base = pl.multiple_of(step * block, block)
    keys = pl.ds(base, band)

    @pl.when(step == 0)
    def _():
        dk_ref[...] = jnp.zeros_like(dk_ref)
        dv_ref[...] = jnp.zeros_like(dv_ref)

    row = lax.broadcasted_iota(jnp.int32, (band, block), 0)
    col = lax.broadcasted_iota(jnp.int32, (band, block), 1)
    allowed = (qid_ref[...] == kid_ref[...]) & (row <= col + (band - block))
    bias = jnp.where(allowed, 0.0, -1e30)
    acc_ref[...] = jnp.zeros_like(acc_ref)
    scale = HEAD**-0.5
    for h in range(HEADS):
        a, b, lanes = head_window(h, width)
        query = jnp.where(lanes, q_ref[:, a:b].astype(F32), 0.0).astype(BF)
        grad = jnp.where(lanes, g_ref[:, a:b].astype(F32), 0.0).astype(BF)
        key = k_ref[keys, a:b]
        scores = mm_nt(key, query) * scale + bias
        e = jnp.exp(scores - jnp.max(scores, axis=0, keepdims=True))
        probs = e * (1.0 / jnp.sum(e, axis=0, keepdims=True))
        grad_probs = mm_nt(v_ref[keys, a:b], grad)
        dv_ref[keys, a:b] += mm(probs.astype(BF), grad)
        dot = jnp.sum(grad_probs * probs, axis=0, keepdims=True)
        grad_scores = (probs * (grad_probs - dot)).astype(BF)
        dk_ref[keys, a:b] += mm(grad_scores, query) * scale
        acc_ref[:, a:b] += jnp.where(lanes, mm_tn(grad_scores, key), 0.0)
    dq_ref[...] = (acc_ref[...] * scale).astype(BF)

    @pl.when(step == pl.num_programs(0) - 1)
    def _():
        prev_ref[0] = dk_ref[0:span, :].astype(BF)
        prev_ref[1] = dv_ref[0:span, :].astype(BF)
        own_ref[0] = dk_ref[span : 2 * span, :]
        own_ref[1] = dv_ref[span : 2 * span, :]


def attend_back(q, k, v, grad, qid, kid, block):
    t, d = q.shape
    band = kid.shape[1]
    whole = pl.BlockSpec((2 * t, d), lambda i: (0, 0))
    rows = pl.BlockSpec((block, d), lambda i: (i, 0))
    pair = pl.BlockSpec((2, t, d), lambda i: (0, 0, 0))
    return pl.pallas_call(
        attend_back_kernel,
        grid=(t // block,),
        in_specs=[
            rows,
            whole,
            whole,
            rows,
            pl.BlockSpec((1, block), lambda i: (0, i)),
            pl.BlockSpec((None, band, 1), lambda i: (i, 0, 0)),
        ],
        out_specs=[rows, pair, pair],
        out_shape=[
            jax.ShapeDtypeStruct((t, d), BF),
            jax.ShapeDtypeStruct((2, t, d), BF),
            jax.ShapeDtypeStruct((2, t, d), F32),
        ],
        scratch_shapes=[
            pltpu.VMEM((block, d), F32),
            pltpu.VMEM((2 * t, d), F32),
            pltpu.VMEM((2 * t, d), F32),
        ],
        compiler_params=params(1),
        name="attend_back",
    )(q, k, v, grad, qid, kid)


def mlp_kernel(
    x_ref, mixed_ref, cot_ref, wo_ref, wf_ref, wp_ref, vec_ref, bfc_ref,
    out_ref, ht_ref, gp_ref, nt_ref, mt_ref, ga_ref, gb_ref, gm_ref, gbfc_ref, sums_ref,
    after_ref, n_ref, oacc_ref, gacc_ref,
):
    chunk, tok = pl.program_id(0), pl.program_id(1)
    last = pl.num_programs(0) - 1
    tb = x_ref.shape[0]
    rows = pl.ds(pl.multiple_of(tok * tb, tb), tb)

    @pl.when(chunk == 0)
    def _():
        mixed = mixed_ref[...]
        after = x_ref[...].astype(F32) + (mm(mixed, wo_ref[...]) + vec_ref[0:1, :])
        normed, _ = standardize(after)
        n = (normed * vec_ref[1:2, :] + vec_ref[2:3, :]).astype(BF)
        after_ref[rows, :] = after
        n_ref[rows, :] = n
        mt_ref[...] = mixed.T
        nt_ref[...] = n.T
        oacc_ref[rows, :] = after + vec_ref[3:4, :]
        gacc_ref[rows, :] = jnp.zeros_like(after)

    @pl.when((chunk == 0) & (tok == 0))
    def _():
        sums_ref[...] = jnp.zeros_like(sums_ref)

    @pl.when(tok == 0)
    def _():
        gbfc_ref[...] = jnp.zeros_like(gbfc_ref)

    pre = mm(n_ref[rows, :], wf_ref[...]) + bfc_ref[...]
    phi = 0.5 + 0.5 * lax.erf(pre * ROOT_HALF)
    hidden = (pre * phi).astype(BF)
    slope = phi + pre * (jnp.exp(-0.5 * pre * pre) * INV_ROOT_2PI)
    cot = cot_ref[...]
    grad_pre = (mm_nt(cot, wp_ref[...]) * slope).astype(BF)
    oacc_ref[rows, :] += mm(hidden, wp_ref[...])
    gacc_ref[rows, :] += mm_nt(grad_pre, wf_ref[...])
    gp_ref[...] = grad_pre
    ht_ref[...] = hidden.T
    gbfc_ref[...] += jnp.sum(grad_pre.astype(F32), axis=0, keepdims=True)

    @pl.when(chunk == last)
    def _():
        out_ref[...] = oacc_ref[rows, :].astype(BF)
        normed, inv = standardize(after_ref[rows, :])
        grad_mid = gacc_ref[rows, :]
        wide_cot = cot.astype(F32)
        grad_after = wide_cot + norm_pullback(grad_mid, normed, inv, vec_ref[1:2, :])
        grad_attn = grad_after.astype(BF)
        ga_ref[...] = grad_after
        gb_ref[...] = grad_attn
        gm_ref[...] = mm_nt(grad_attn, wo_ref[...]).astype(BF)
        sums_ref[0:1, :] += jnp.sum(grad_mid * normed, axis=0, keepdims=True)
        sums_ref[1:2, :] += jnp.sum(grad_mid, axis=0, keepdims=True)
        sums_ref[2:3, :] += jnp.sum(grad_attn.astype(F32), axis=0, keepdims=True)
        sums_ref[3:4, :] += jnp.sum(wide_cot, axis=0, keepdims=True)


def mlp(x, mixed, cot, wa, wf, wp, vec, bfc, tb):
    t, d = x.shape
    nb, chunks = t // tb, wf.shape[0]
    first = lambda c, i: (jnp.where(c == 0, i, nb - 1), 0)
    first_t = lambda c, i: (0, jnp.where(c == 0, i, nb - 1))
    final = lambda c, i: (jnp.where(c == chunks - 1, i, 0), 0)
    rows = lambda index: pl.BlockSpec((tb, d), index)
    per_chunk = pl.BlockSpec((None, d, d), lambda c, i: (c, 0, 0))
    f32 = jax.ShapeDtypeStruct((t, d), F32)
    bf = jax.ShapeDtypeStruct((t, d), BF)
    bft = jax.ShapeDtypeStruct((d, t), BF)
    return pl.pallas_call(
        mlp_kernel,
        grid=(chunks, nb),
        in_specs=[
            rows(first),
            rows(first),
            rows(lambda c, i: (i, 0)),
            pl.BlockSpec((None, d, d), lambda c, i: (3, 0, 0)),
            per_chunk,
            per_chunk,
            pl.BlockSpec(vec.shape, lambda c, i: (0, 0)),
            pl.BlockSpec((None, 1, d), lambda c, i: (c, 0, 0)),
        ],
        out_specs=[
            rows(final),
            pl.BlockSpec((None, d, tb), lambda c, i: (c, 0, i)),
            pl.BlockSpec((None, tb, d), lambda c, i: (c, i, 0)),
            pl.BlockSpec((d, tb), first_t),
            pl.BlockSpec((d, tb), first_t),
            rows(final),
            rows(final),
            rows(final),
            pl.BlockSpec((None, 1, d), lambda c, i: (c, 0, 0)),
            pl.BlockSpec((8, d), lambda c, i: (0, 0)),
        ],
        out_shape=[
            bf,
            jax.ShapeDtypeStruct((chunks, d, t), BF),
            jax.ShapeDtypeStruct((chunks, t, d), BF),
            bft,
            bft,
            f32,
            bf,
            bf,
            jax.ShapeDtypeStruct((chunks, 1, d), F32),
            jax.ShapeDtypeStruct((8, d), F32),
        ],
        scratch_shapes=[
            pltpu.VMEM((t, d), F32),
            pltpu.VMEM((t, d), BF),
            pltpu.VMEM((t, d), F32),
            pltpu.VMEM((t, d), F32),
        ],
        compiler_params=params(2),
        name="mlp",
    )(x, mixed, cot, wa, wf, wp, vec, bfc)


def qkv_back_kernel(
    dq_ref, own_ref, next_ref, gb_ref, x_ref, ga_ref, wq_ref, wk_ref, wv_ref, vec_ref,
    dx_ref, gp_ref, sums_ref,
):
    @pl.when(pl.program_id(0) == 0)
    def _():
        sums_ref[...] = jnp.zeros_like(sums_ref)

    dq = dq_ref[...]
    dk = (own_ref[0] + next_ref[0].astype(F32)).astype(BF)
    dv = (own_ref[1] + next_ref[1].astype(F32)).astype(BF)
    gp_ref[0] = dq
    gp_ref[1] = dk
    gp_ref[2] = dv
    gp_ref[3] = gb_ref[...]
    grad = mm_nt(dq, wq_ref[...]) + mm_nt(dk, wk_ref[...]) + mm_nt(dv, wv_ref[...])
    normed, inv = standardize(x_ref[...].astype(F32))
    dx_ref[...] = ga_ref[...] + norm_pullback(grad, normed, inv, vec_ref[0:1, :])
    sums_ref[0:1, :] += jnp.sum(dq.astype(F32), axis=0, keepdims=True)
    sums_ref[1:2, :] += jnp.sum(dv.astype(F32), axis=0, keepdims=True)
    sums_ref[2:3, :] += jnp.sum(grad * normed, axis=0, keepdims=True)
    sums_ref[3:4, :] += jnp.sum(grad, axis=0, keepdims=True)


def qkv_back(dq, own, nxt, gb, x, ga, wa, vec, tb):
    t, d = x.shape
    rows = pl.BlockSpec((tb, d), lambda i: (i, 0))
    pair = pl.BlockSpec((2, tb, d), lambda i: (0, i, 0))
    weight = lambda s: pl.BlockSpec((None, d, d), lambda i: (s, 0, 0))
    return pl.pallas_call(
        qkv_back_kernel,
        grid=(t // tb,),
        in_specs=[
            rows, pair, pair, rows, rows, rows,
            weight(0), weight(1), weight(2),
            pl.BlockSpec(vec.shape, lambda i: (0, 0)),
        ],
        out_specs=[
            rows,
            pl.BlockSpec((4, tb, d), lambda i: (0, i, 0)),
            pl.BlockSpec((8, d), lambda i: (0, 0)),
        ],
        out_shape=[
            jax.ShapeDtypeStruct((t, d), F32),
            jax.ShapeDtypeStruct((4, t, d), BF),
            jax.ShapeDtypeStruct((8, d), F32),
        ],
        compiler_params=params(1),
        name="qkv_back",
    )(dq, own, nxt, gb, x, ga, wa, wa, wa, vec)


def weight_grad_kernel(place_ref, *refs):
    *pairs, out_ref = refs
    total = mm(pairs[0][...], pairs[1][...])
    for i in range(2, len(pairs), 2):
        total += mm(pairs[i][...], pairs[i + 1][...])
    out_ref[...] = total.astype(BF)


def weight_grad(pairs, left_of, right_of, place):
    m, t = pairs[0][0].shape[-2:]
    n = pairs[0][1].shape[-1]
    specs, operands = [], []
    for left, right in pairs:
        specs.append(pl.BlockSpec((None, m, t), lambda r, s: (left_of(r, r ^ s[0]), 0, 0)))
        specs.append(pl.BlockSpec((None, t, n), lambda r, s: (right_of(r, r ^ s[0]), 0, 0)))
        operands += [left, right]
    return pl.pallas_call(
        weight_grad_kernel,
        grid_spec=pltpu.PrefetchScalarGridSpec(
            num_scalar_prefetch=1,
            grid=(4,),
            in_specs=specs,
            out_specs=pl.BlockSpec((None, m, n), lambda r, s: (r, 0, 0)),
        ),
        out_shape=jax.ShapeDtypeStruct((4, m, n), BF),
        compiler_params=params(1),
        name="weight_grad",
    )(place, *operands)


def assemble_kernel(swapped, place_ref, own_ref, mine_ref, other_ref, out_ref, sems):
    chip, core, depth = place_ref[0], place_ref[1], place_ref[2]
    chunks, block, _ = own_ref.shape
    depths = mine_ref.shape[1] + 1
    piece = mine_ref.shape[2]
    skip = 2 * piece - block

    def target(chunk, z, start, size):
        row = pl.multiple_of((chunk if swapped else z) * block, 8) + start
        return out_ref.at[z if swapped else chunk, pl.ds(pl.multiple_of(row, 8), size), :]

    def run(halves):
        copies = []
        for r in range(chunks):
            chunk = r ^ chip
            copies.append((own_ref.at[chunk], target(chunk, depth, 0, block)))
            for d in range(1, depths):
                z = lax.rem(depth - d + depths, depths)
                copies.append(
                    (halves[0].at[r, d - 1], target(chunk, z, 0, piece))
                )
                copies.append(
                    (
                        halves[1].at[r, d - 1, pl.ds(skip, piece - skip), :],
                        target(chunk, z, piece, piece - skip),
                    )
                )
        started = [
            pltpu.make_async_copy(source, there, sems.at[i])
            for i, (source, there) in enumerate(copies)
        ]
        for copy in started:
            copy.start()
        for copy in started:
            copy.wait()

    @pl.when(core == 0)
    def _():
        run((mine_ref, other_ref))

    @pl.when(core == 1)
    def _():
        run((other_ref, mine_ref))


def assemble(own, mine, other, place, swapped):
    chunks, block, width = own.shape
    depths = mine.shape[1] + 1
    shape = (depths, chunks * block, width) if swapped else (chunks, depths * block, width)
    hbm = pl.BlockSpec(memory_space=pl.ANY)
    return pl.pallas_call(
        functools.partial(assemble_kernel, swapped),
        in_specs=[pl.BlockSpec(memory_space=pltpu.SMEM), hbm, hbm, hbm],
        out_specs=pl.BlockSpec(memory_space=pltpu.VMEM),
        out_shape=jax.ShapeDtypeStruct(shape, own.dtype),
        scratch_shapes=[pltpu.SemaphoreType.DMA((chunks * (2 * depths - 1),))],
        compiler_params=pltpu.CompilerParams(vmem_limit_bytes=VMEM_LIMIT),
        name="assemble",
    )(place, own, mine, other)


def flip(value, bit):
    count = lax.axis_size("wide")
    return lax.ppermute(value, "wide", [(i, i ^ bit) for i in range(count)])


def along(value, distance):
    count = lax.axis_size("narrow")
    return lax.ppermute(value, "narrow", [(i, (i + distance) % count) for i in range(count)])


def from_behind(value, distance):
    count = lax.axis_size("narrow")
    route = [(i - distance, i) for i in range(count) if 0 <= i - distance < count]
    return lax.ppermute(value, "narrow", route)


def add_low(*terms):
    total = terms[0].astype(F32)
    for term in terms[1:]:
        total = total + term.astype(F32)
    return total.astype(BF)


def plane_gather(value):
    half = value.shape[-2] // 2
    across_x = flip(value, 2)
    across_y = flip(value, 4)
    upper = flip(across_x[..., :half, :], 4)
    lower = flip(across_y[..., half:, :], 2)
    mine = jnp.stack([value, across_x, across_y, jnp.concatenate([upper, lower], axis=-2)])
    return mine, flip(mine, 1)


def plane_scatter(grads):
    half = grads.shape[-2] // 2
    upper = flip(grads[3][..., :half, :], 2)
    lower = flip(grads[3][..., half:, :], 4)
    to_x = jnp.concatenate(
        [grads[1][..., :half, :], add_low(grads[1][..., half:, :], lower)], axis=-2
    )
    to_y = jnp.concatenate(
        [add_low(grads[2][..., :half, :], upper), grads[2][..., half:, :]], axis=-2
    )
    return add_low(grads[0], flip(to_x, 2), flip(to_y, 4))


def depth_scatter(grads):
    parts = [grads[0]]
    for d in range(1, grads.shape[0]):
        parts.append(along(grads[d], d))
    return add_low(*parts)


def roll_from(value, start, axis):
    count = value.shape[axis]
    twice = jnp.concatenate([value, lax.slice_in_dim(value, 0, count - 1, axis=axis)], axis=axis)
    return lax.dynamic_slice_in_dim(twice, start, count, axis=axis)


def shards(
    inputs, cell_lengths, w_qkv, w_out, w_fc, w_proj, b_query, b_value, b_out, b_fc, b_proj,
    gain_attn, shift_attn, gain_mlp, shift_mlp, cotangent,
):
    _, span, d = inputs.shape
    depths = lax.axis_size("narrow")
    chips = lax.axis_size("wide") // 2
    block = w_qkv.shape[0]
    chunks = w_fc.shape[1] // d
    direct = chips == chunks == depths == 4 and block % 8 == 0
    wide_index = lax.axis_index("wide")
    chip, core = wide_index // 2, wide_index % 2
    depth = lax.axis_index("narrow")
    tb = min(256, span)
    qb = 128
    band = span + qb

    x_own = inputs.reshape(span, d)
    cot = cotangent.reshape(span, d)
    x_prev = from_behind(x_own, 1)

    own_a = jnp.stack([w_qkv[:, i * d : (i + 1) * d] for i in range(3)] + [w_out])
    own_f = jnp.stack([w_fc[:, i * d : (i + 1) * d] for i in range(chunks)])
    small = jnp.concatenate(
        [b_query, b_value, b_out, b_proj, gain_attn, shift_attn, gain_mlp, shift_mlp, b_fc]
    ).reshape(1, -1)
    if direct:
        piece = -(-block // 16) * 8
        place = jnp.stack([chip, core, depth]).astype(jnp.int32)
        own_p = w_proj.reshape(chunks, block, d)

        def gather(own, swapped):
            part = lax.dynamic_slice(own, (chip, core * (block - piece), 0), (1, piece, d))[0]
            foreign = jnp.stack([along(part, k) for k in range(1, depths)])
            mine, other = plane_gather(foreign)
            return assemble(own, mine, other, place, swapped)

        wa = gather(own_a, False)
        wf = gather(own_f, False)
        wp = gather(own_p, True)
        arrived = [small] + [along(small, k) for k in range(1, depths)]
        order = jnp.concatenate([arrived[(-e) % depths] for e in range(2 * depths)])
        small = lax.dynamic_slice_in_dim(order, (depths - depth) % depths, depths, axis=0)
    else:
        everything = lambda value, axis: lax.all_gather(value, "narrow", axis=axis, tiled=True)
        wa = everything(own_a, 1)
        wf = everything(own_f, 1)
        wp = everything(w_proj, 0).reshape(chunks, d, d)
        small = everything(small, 0)
    small = small.astype(F32)
    vectors = [small[:, i * block : (i + 1) * block].reshape(1, d) for i in range(8)]
    bias_q, bias_v, bias_o, bias_p, gain_1, shift_1, gain_2, shift_2 = vectors
    bias_f = small[:, 8 * block :].reshape(chunks, 1, d)
    vec_1 = jnp.concatenate([gain_1, shift_1, bias_q, bias_v] + [jnp.zeros_like(bias_q)] * 4)
    vec_2 = jnp.concatenate([bias_o, gain_2, shift_2, bias_p] + [jnp.zeros_like(bias_q)] * 4)

    starts = jnp.cumsum(cell_lengths, axis=-1) - cell_lengths
    pos = (depth - 1) * span + jnp.arange(2 * span, dtype=jnp.int32)
    ids = jnp.sum((starts <= pos[:, None]).astype(jnp.int32), axis=-1) - 1
    query_ids = ids[span:]
    key_ids = jnp.stack([ids[i * qb : i * qb + band] for i in range(span // qb)])

    q, k, v, nt_1 = ln_qkv(x_prev, x_own, wa, vec_1, tb)
    mixed = attend(q, k, v, query_ids[:, None], key_ids[:, None, :], qb)
    out, ht, gp_f, nt_2, mt, grad_after, grad_attn, grad_mixed, grad_bfc, sums_2 = mlp(
        x_own, mixed, cot, wa, wf, wp, vec_2, bias_f, tb
    )
    dq, kv_prev, kv_own = attend_back(
        q, k, v, grad_mixed, query_ids[None, :], key_ids[:, :, None], qb
    )
    kv_next = from_behind(kv_prev, -1)
    dx, gp_a, sums_1 = qkv_back(dq, kv_own, kv_next, grad_attn, x_own, grad_after, wa, vec_1, tb)

    left_a = jnp.stack([nt_1, mt])
    if direct:
        def halves(value):
            value = roll_from(value, depth, 1)
            take = lambda at: lax.dynamic_slice_in_dim(value, at * (block - piece), piece, axis=2)
            flat = lambda a: a.reshape(a.shape[0], depths * piece, span)
            return flat(take(core)), flip(flat(take(1 - core)), 1)

        def reduce(pairs, left_of, right_of):
            grads = weight_grad(pairs, left_of, right_of, place)
            grads = plane_scatter(grads.reshape(chunks, depths, piece, d))
            mine, other = plane_gather(depth_scatter(grads))
            first = jnp.where(core == 0, mine, other)
            second = jnp.where(core == 0, other, mine)[:, 2 * piece - block :, :]
            both = jnp.concatenate([first, second], axis=1)
            return [
                lax.dynamic_index_in_dim(both, i ^ chip, 0, keepdims=False).astype(F32)
                for i in range(chunks)
            ]

        by_chip = jnp.stack(
            [
                lax.dynamic_index_in_dim(
                    ht.reshape(depths, chunks, block, span), r ^ chip, 1, keepdims=False
                )
                for r in range(chunks)
            ]
        )
        here, there = halves(by_chip)
        cots = cot[None]
        shard_p = reduce(
            [(here, cots), (there, flip(cots, 1))], lambda r, c: r, lambda r, c: 0
        )
        here, there = halves(nt_2.reshape(1, depths, block, span))
        shard_f = reduce(
            [(here, gp_f), (there, flip(gp_f, 1))], lambda r, c: 0, lambda r, c: c
        )
        here, there = halves(left_a.reshape(2, depths, block, span))
        shard_a = reduce(
            [(here, gp_a), (there, flip(gp_a, 1))], lambda r, c: c // 3, lambda r, c: c
        )
        shard_p = jnp.concatenate(shard_p, axis=0)
    else:
        zero = jnp.zeros((1,), jnp.int32)

        def reduce(left, right, left_of, right_of, axis):
            grads = weight_grad([(left, right)], left_of, right_of, zero).astype(F32)
            grads = lax.psum(grads, "wide")
            return lax.psum_scatter(grads, "narrow", scatter_dimension=axis, tiled=True)

        shard_p = lax.psum(
            weight_grad([(ht, cot[None])], lambda r, c: c, lambda r, c: 0, zero).astype(F32), "wide"
        )
        shard_p = lax.psum_scatter(
            shard_p.reshape(chunks * d, d), "narrow", scatter_dimension=0, tiled=True
        )
        shard_f = reduce(nt_2[None], gp_f, lambda r, c: 0, lambda r, c: c, 1)
        shard_a = reduce(left_a, gp_a, lambda r, c: c // 3, lambda r, c: c, 1)
    shard_qkv = jnp.concatenate([shard_a[i] for i in range(3)], axis=1)
    shard_fc = jnp.concatenate([shard_f[i] for i in range(chunks)], axis=1)

    rows = [sums_1[0], sums_1[1], sums_2[2], sums_2[3], sums_1[2], sums_1[3], sums_2[0], sums_2[1]]
    packed = jnp.concatenate(
        [r.reshape(depths, block) for r in rows] + [grad_bfc.reshape(depths, chunks * block)], axis=1
    )
    packed = lax.psum(packed, ("wide", "narrow"))
    packed = lax.dynamic_index_in_dim(packed, depth, 0, keepdims=False)
    small_grads = [packed[i * block : (i + 1) * block] for i in range(8)]
    g_bq, g_bv, g_bo, g_bp, g_g1, g_s1, g_g2, g_s2 = small_grads
    return (
        out.reshape(inputs.shape),
        dx.reshape(inputs.shape),
        shard_qkv,
        shard_a[3],
        shard_fc,
        shard_p,
        g_bq,
        g_bv,
        g_bo,
        packed[8 * block :],
        g_bp,
        g_g1,
        g_s1,
        g_g2,
        g_s2,
    )


def solution(mesh):
    rows, flat = P("narrow", None), P("narrow")
    tokens = P("wide", "narrow", None)
    in_specs = (tokens, P("wide", None)) + (rows,) * 4 + (flat,) * 9 + (tokens,)
    out_specs = (tokens, tokens) + (rows,) * 4 + (flat,) * 9
    return jax.shard_map(shards, mesh=mesh, in_specs=in_specs, out_specs=out_specs, check_vma=False)
```

time: 2130 us -> 804 us (0.38)
  blocking collectives: 995 us -> 43.6 us
  matrix products: 233 us -> 0 us
  Pallas kernels: 0 us -> 219 us
  waiting for transfers between devices: 443 us -> 255 us
  local copies, waits for them, and re-layouts: 261 us -> 100 us
  other arithmetic: 173 us -> 52.8 us
  starting transfers between devices: 4.19 us -> 121 us
    unnamed x2 -> x0, blocking collectives: 973 us -> none
    all_gather x7 -> x0, waiting for transfers between devices: 359 us -> none  [the longest x1 147 us: shards(): lax.all_gather(w_proj, 'narrow', axis=0, tiled=True)]
    dot_general x18 -> x0, matrix products: 233 us -> none  [the longest x1 33.5 us: shards(): jnp.dot(mlp_in, mat_fc, preferred_element_type=jnp.float32) + bias_fc]
    pallas_call x0 -> x11, Pallas kernels: none -> 219 us  [the longest x1 56.8 us: attend_back(): pl.pallas_call(attend_back_kernel, grid=(t // block,), in_specs=[rows, wh...]
    reshape x27 -> x10, local copies, waits for them, and re-layouts: 223 us -> 5.96 us  [the longest x8 5.33 us: shards(): small[:, i * block:(i + 1) * block].reshape(1, d)]
    ppermute x2 -> x71, waiting for transfers between devices: 81 us -> 255 us  [the longest x48 158 us: flip(): return lax.ppermute(value, 'wide', [(i, i ^ bit) for i in range(count)])]
    ppermute x2 -> x71, starting transfers between devices: 3.91 us -> 121 us  [the longest x21 67.1 us: along(): lax.ppermute(value, 'narrow', [(i, (i + distance) % count) for i in range...]
    reshape x8 -> x0, other arithmetic: 77.6 us -> none  [the longest x1 29.4 us: shards(): shard_qkv = reduced[0].reshape(w_qkv.shape)]
  transfers between devices with their start and end apart: 9 -> 71, of which waited for: 6 -> 29; matrix products, arithmetic and copies ran while one was open for 19% -> 16% of each run, Pallas kernels for 0% -> 20%
where the time goes in v1:
time: 804 us; the launch traced here: 794 us
  waiting for transfers between devices  255 us (32%)
  Pallas kernels  219 us (27%)
  starting transfers between devices  121 us (15%)
  local copies, waits for them, and re-layouts  100 us (12%)
  other arithmetic  52.8 us (7%)
  blocking collectives  43.6 us (5%)
    ppermute x48, waiting for transfers between devices, flip(): return lax.ppermute(value, 'wide', [(i, i ^ bit) for i in range(count)])  158 us
    ppermute x21, waiting for transfers between devices, along(): lax.ppermute(value, 'narrow', [(i, (i + distance) % count) for i in range...  68.1 us
    ppermute x21, starting transfers between devices, along(): lax.ppermute(value, 'narrow', [(i, (i + distance) % count) for i in range...  67.1 us
    pallas_call x1, Pallas kernels, attend_back(): pl.pallas_call(attend_back_kernel, grid=(t // block,), in_specs=[rows, wh...  56.8 us
    ppermute x48, starting transfers between devices, flip(): return lax.ppermute(value, 'wide', [(i, i ^ bit) for i in range(count)])  49.6 us
    psum x1, blocking collectives, shards(): packed = lax.psum(packed, ('wide', 'narrow'))  43.6 us
    pallas_call x1, Pallas kernels, mlp(): pl.pallas_call(mlp_kernel, grid=(chunks, nb), in_specs=[rows(first), rows...  43.5 us
    pallas_call x3, Pallas kernels, weight_grad(): pl.pallas_call(weight_grad_kernel, grid_spec=pltpu.PrefetchScalarGridSpec...  33.2 us
  transfers between devices with their start and end apart: 71, of which 29 were waited for; matrix products, arithmetic and copies ran while one was open for 16% of the time, Pallas kernels for 20%

profile of v1, /device:TPU:0, one launch (start us, length us, event | category | flops | bytes accessed | tf_op | source)
XLA Modules:
  0.0 793.8 jit_solution(9096930827389065600)
XLA Ops:
  18.0 11.8 %collective-permute-done.21 = bf16[144,1120]{1,0:T(8,128)(2,1)S(1)} collective-permute-done((bf16[144,1120]{1,0:T(8,128)(2,1)S(1)}, bf16[144,1120]{1,0:T(8,128)(2,1)S(1)}, u32[]{:S(2)}, u32[]{:S(2)}) %collective-permute-start.21) | collective-permute-done | bytes 322592 | tf_op jit(solution)/shard_map/ppermute | solution.py:498
  31.8 21.9 %collective-permute-start.1 = (bf16[144,1120]{1,0:T(8,128)(2,1)S(1)}, bf16[144,1120]{1,0:T(8,128)(2,1)S(1)}, u32[]{:S(2)}, u32[]{:S(2)}) collective-permute-start(bf16[144,1120]{1,0:T(8,128)(2,1)S(1)} %dynamic-slice_bitcast_fusion.6), channel_id=1, source_target_pairs={{0,1},{1,2},{2,3},{3,0},{4,5},{5,6},{6,7},{7,4},{8,9},{9,10},{10,1... | collective-permute-start | bytes 967688 | tf_op jit(solution)/shard_map/ppermute | solution.py:498
  59.2 12.5 %collective-permute-done.13 = bf16[144,1120]{1,0:T(8,128)(2,1)S(1)} collective-permute-done((bf16[144,1120]{1,0:T(8,128)(2,1)S(1)}, bf16[144,1120]{1,0:T(8,128)(2,1)S(1)}, u32[]{:S(2)}, u32[]{:S(2)}) %collective-permute-start.13) | collective-permute-done | bytes 322592 | tf_op jit(solution)/shard_map/ppermute | solution.py:498
  77.6 8.3 %collective-permute-done.2 = bf16[144,1120]{1,0:T(8,128)(2,1)S(1)} collective-permute-done((bf16[144,1120]{1,0:T(8,128)(2,1)S(1)}, bf16[144,1120]{1,0:T(8,128)(2,1)S(1)}, u32[]{:S(2)}, u32[]{:S(2)}) %collective-permute-start.2) | collective-permute-done | bytes 322592 | tf_op jit(solution)/shard_map/ppermute | solution.py:498
  91.7 7.6 collective-permute-done.24
  102.6 18.0 %collective-permute-done.16 = bf16[3,144,1120]{2,1,0:T(8,128)(2,1)S(1)} collective-permute-done((bf16[3,144,1120]{2,1,0:T(8,128)(2,1)S(1)}, bf16[3,144,1120]{2,1,0:T(8,128)(2,1)S(1)}, u32[]{:S(2)}, u32[]{:S(2)}) %collective-permute-start.16) | collective-permute-done | bytes 967712 | tf_op jit(solution)/shard_map/ppermute | solution.py:493
  123.9 18.0 %collective-permute-done.5 = bf16[3,144,1120]{2,1,0:T(8,128)(2,1)S(1)} collective-permute-done((bf16[3,144,1120]{2,1,0:T(8,128)(2,1)S(1)}, bf16[3,144,1120]{2,1,0:T(8,128)(2,1)S(1)}, u32[]{:S(2)}, u32[]{:S(2)}) %collective-permute-start.5) | collective-permute-done | bytes 967712 | tf_op jit(solution)/shard_map/ppermute | solution.py:493
  143.5 9.1 %collective-permute-done.25 = bf16[3,72,1120]{2,1,0:T(8,128)(2,1)S(1)} collective-permute-done((bf16[3,72,1120]{2,1,0:T(8,128)(2,1)S(1)}, bf16[3,72,1120]{2,1,0:T(8,128)(2,1)S(1)}, u32[]{:S(2)}, u32[]{:S(2)}) %collective-permute-start.25) | collective-permute-done | bytes 483872 | tf_op jit(solution)/shard_map/ppermute | solution.py:493
  156.5 13.9 %collective-permute-done.6 = bf16[3,72,1120]{2,1,0:T(8,128)(2,1)S(1)} collective-permute-done((bf16[3,72,1120]{2,1,0:T(8,128)(2,1)S(1)}, bf16[3,72,1120]{2,1,0:T(8,128)(2,1)S(1)}, u32[]{:S(2)}, u32[]{:S(2)}) %collective-permute-start.6) | collective-permute-done | bytes 483872 | tf_op jit(solution)/shard_map/ppermute | solution.py:493
  188.1 22.3 %collective-permute-done.11 = bf16[1,3360]{1,0:T(2,128)(2,1)S(1)} collective-permute-done((bf16[1,3360]{1,0:T(2,128)(2,1)S(1)}, bf16[1,3360]{1,0:T(2,128)(2,1)S(1)}, u32[]{:S(2)}, u32[]{:S(2)}) %collective-permute-start.11) | collective-permute-done | bytes 6752 | tf_op jit(solution)/shard_map/ppermute | solution.py:498
  231.6 9.2 %assemble.3.wq_ref.wk_ref.wv_ref.wo_ref = bf16[4,1120,1120]{2,1,0:T(8,128)(2,1)} custom-call(s32[3]{0:T(128)} %pad_add_fusion.1.place_ref, bf16[4,280,1120]{2,1,0:T(8,128)(2,1)} %copy-done.1, bf16[4,3,144,1120]{3,2,1,0:T(8,128)(2,1)} %pad_maximum_fusion.4.mine_ref, bf16[4,3,144,1120]{3,2,1,0:T(8,128)(2,1)} %collective-permute-done.8.other_ref), custom_call_target="tpu_custom_call" | custom-call | tf_op jit(solution)/shard_map/assemble/pallas_call | solution.py:480
  240.8 15.9 %ln_qkv.1 = (bf16[512,1120]{1,0:T(8,128)(2,1)}, bf16[1024,1120]{1,0:T(8,128)(2,1)}, bf16[1024,1120]{1,0:T(8,128)(2,1)}, bf16[1120,512]{1,0:T(8,128)(2,1)}) custom-call(bf16[512,1120]{1,0:T(8,128)(2,1)} %copy.64.xp_ref, bf16[512,1120]{1,0:T(8,128)(2,1)} %bitcast.174, bf16[4,1120,1120]{2,1,0:T(8,128)(2,1)} %assemble.3.wq_ref.wk_ref.wv_ref.wo_ref, ...), custom_call_target="tpu_custom_call" | custom-call | tf_op jit(solution)/shard_map/ln_qkv/pallas_call | solution.py:81
  256.7 29.5 %attend.1.mixed_ref = bf16[512,1120]{1,0:T(8,128)(2,1)} custom-call(bf16[512,1120]{1,0:T(8,128)(2,1)} %get-tuple-element.35.q_ref, bf16[1024,1120]{1,0:T(8,128)(2,1)} %get-tuple-element.36.k_ref, bf16[1024,1120]{1,0:T(8,128)(2,1)} %get-tuple-element.37.v_ref, s32[512,1]{1,0:T(8,128)} %copy.65.qid_ref, s32[4,1,640]{2,1,0:T(1,128)} %broadcast_in_dim.14.kid_ref), custom_call_target="tpu_custom_call" | custom-call | tf_op jit(solution)/shard_map/attend/pallas_call | solution.py:133
  286.2 8.6 %assemble.5.wp_ref = bf16[4,1120,1120]{2,1,0:T(8,128)(2,1)} custom-call(s32[3]{0:T(128)} %pad_add_fusion.1.place_ref, bf16[4,280,1120]{2,1,0:T(8,128)(2,1)} %bitcast.202, bf16[4,3,144,1120]{3,2,1,0:T(8,128)(2,1)} %pad_maximum_fusion.6.mine_ref, bf16[4,3,144,1120]{3,2,1,0:T(8,128)(2,1)} %collective-permute-done.27.other_ref), custom_call_target="tpu_custom_call" | custom-call | tf_op jit(solution)/shard_map/assemble/pallas_call | solution.py:480
  294.9 8.8 %assemble.4.wf_ref = bf16[4,1120,1120]{2,1,0:T(8,128)(2,1)} custom-call(s32[3]{0:T(128)} %pad_add_fusion.1.place_ref, bf16[4,280,1120]{2,1,0:T(8,128)(2,1)} %copy-done, bf16[4,3,144,1120]{3,2,1,0:T(8,128)(2,1)} %pad_maximum_fusion.5.mine_ref, bf16[4,3,144,1120]{3,2,1,0:T(8,128)(2,1)} %collective-permute-done.19.other_ref), custom_call_target="tpu_custom_call" | custom-call | tf_op jit(solution)/shard_map/assemble/pallas_call | solution.py:480
  303.7 43.5 %mlp.1 = (bf16[512,1120]{1,0:T(8,128)(2,1)}, bf16[4,1120,512]{2,1,0:T(8,128)(2,1)}, bf16[4,512,1120]{2,1,0:T(8,128)(2,1)}, bf16[1120,512]{1,0:T(8,128)(2,1)}, bf...) custom-call(bf16[512,1120]{1,0:T(8,128)(2,1)} %bitcast.175, ...), custom_call_target="tpu_custom_call" | custom-call | tf_op jit(solution)/shard_map/mlp/pallas_call | solution.py:300
  364.0 10.6 %weight_grad.5 = bf16[4,576,1120]{2,1,0:T(8,128)(2,1)} custom-call(s32[3]{0:T(128)} %pad_add_fusion.1.place_ref, bf16[4,576,512]{2,1,0:T(8,128)(2,1)} %bitcast.178, bf16[1,512,1120]{2,1,0:T(8,128)(2,1)} %copy.66.refs_1_, bf16[4,576,512]{2,1,0:T(8,128)(2,1)} %collective-permute-done.57.refs_2_, bf16[1,512,1120]{2,1,0:T(8,128)(2,1)} %copy.75.refs_3_), custom_call_target="tpu_custom_call" | custom-call | tf_op jit(solution)/shard_map/weight_grad/pallas_call | solution.py:416
  381.1 6.6 copy.72
  389.3 56.8 %attend_back.1 = (bf16[512,1120]{1,0:T(8,128)(2,1)}, bf16[2,512,1120]{2,1,0:T(8,128)(2,1)}, f32[2,512,1120]{2,1,0:T(8,128)}) custom-call(bf16[512,1120]{1,0:T(8,128)(2,1)} %get-tuple-element.35.q_ref, bf16[1024,1120]{1,0:T(8,128)(2,1)} %get-tuple-element.36.k_ref, bf16[1024,1120]{1,0:T(8,128)(2,1)} %get-tuple-element.37.v_ref, ...), custom_call_target="tpu_custom_call" | custom-call | tf_op jit(solution)/shard_map/attend_back/pallas_call | solution.py:202
  457.4 13.2 %collective-permute-done.61 = bf16[4,72,1120]{2,1,0:T(8,128)(2,1)S(1)} collective-permute-done((bf16[4,72,1120]{2,1,0:T(8,128)(2,1)S(1)}, bf16[4,72,1120]{2,1,0:T(8,128)(2,1)S(1)}, u32[]{:S(2)}, u32[]{:S(2)}) %collective-permute-start.61) | collective-permute-done | bytes 645152 | tf_op jit(solution)/shard_map/ppermute | solution.py:493
  476.2 28.5 %collective-permute-done.28 = bf16[2,512,1120]{1,2,0:T(8,128)(2,1)} collective-permute-done((bf16[2,512,1120]{1,2,0:T(8,128)(2,1)}, bf16[2,512,1120]{1,2,0:T(8,128)(2,1)}, u32[]{:S(2)}, u32[]{:S(2)}) %collective-permute-start.28) | collective-permute-done | bytes 2293792 | tf_op jit(solution)/shard_map/ppermute | solution.py:504
  509.0 13.3 %qkv_back.1 = (f32[512,1120]{1,0:T(8,128)}, bf16[4,512,1120]{2,1,0:T(8,128)(2,1)}, f32[8,1120]{1,0:T(8,128)}) custom-call(bf16[512,1120]{1,0:T(8,128)(2,1)} %get-tuple-element.40.dq_ref, f32[2,512,1120]{2,1,0:T(8,128)} %get-tuple-element.41.own_ref, bf16[2,512,1120]{2,1,0:T(8,128)(2,1)} %copy.69.next_ref, bf16[512,1120]{1,0:T(8,128)(2,1)} %get-tuple-element.43.gb_ref, ...), custom_call_target="tpu_custom_call" | custom-call | tf_op jit(solution)/shard_map/qkv_back/pallas_call | solution.py:377
  522.3 6.6 copy.70
  536.0 6.6 copy.73.refs_3_
  543.4 11.1 %weight_grad.4 = bf16[4,576,1120]{2,1,0:T(8,128)(2,1)} custom-call(s32[3]{0:T(128)} %pad_add_fusion.1.place_ref, bf16[1,576,512]{2,1,0:T(8,128)(2,1)} %bitcast.209, bf16[4,512,1120]{2,1,0:T(8,128)(2,1)} %get-tuple-element.50.refs_1_, bf16[1,576,512]{2,1,0:T(8,128)(2,1)} %copy-done.30, bf16[4,512,1120]{2,1,0:T(8,128)(2,1)} %copy.73.refs_3_), custom_call_target="tpu_custom_call" | custom-call | tf_op jit(solution)/shard_map/weight_grad/pallas_call | solution.py:416
  564.4 10.1 %collective-permute-done.45 = bf16[4,72,1120]{2,1,0:T(8,128)(2,1)S(1)} collective-permute-done((bf16[4,72,1120]{2,1,0:T(8,128)(2,1)S(1)}, bf16[4,72,1120]{2,1,0:T(8,128)(2,1)S(1)}, u32[]{:S(2)}, u32[]{:S(2)}) %collective-permute-start.45) | collective-permute-done | bytes 645152 | tf_op jit(solution)/shard_map/ppermute | solution.py:493
  596.7 11.5 %weight_grad.3 = bf16[4,576,1120]{2,1,0:T(8,128)(2,1)} custom-call(s32[3]{0:T(128)} %pad_add_fusion.1.place_ref, bf16[2,576,512]{2,1,0:T(8,128)(2,1)} %bitcast.197, bf16[4,512,1120]{2,1,0:T(8,128)(2,1)} %get-tuple-element.48.refs_1_, bf16[2,576,512]{2,1,0:T(8,128)(2,1)} %collective-permute-done.29.refs_2_, bf16[4,512,1120]{2,1,0:T(8,128)(2,1)} %copy.71.refs_3_), custom_call_target="tpu_custom_call" | custom-call | tf_op jit(solution)/shard_map/weight_grad/pallas_call | solution.py:416
  622.8 11.2 %collective-permute-done.31 = bf16[4,72,1120]{2,1,0:T(8,128)(2,1)S(1)} collective-permute-done((bf16[4,72,1120]{2,1,0:T(8,128)(2,1)S(1)}, bf16[4,72,1120]{2,1,0:T(8,128)(2,1)S(1)}, u32[]{:S(2)}, u32[]{:S(2)}) %collective-permute-start.31) | collective-permute-done | bytes 645152 | tf_op jit(solution)/shard_map/ppermute | solution.py:493
  639.2 10.9 %collective-permute-done.50 = bf16[144,1120]{1,0:T(8,128)(2,1)S(1)} collective-permute-done((bf16[144,1120]{1,0:T(8,128)(2,1)S(1)}, bf16[144,1120]{1,0:T(8,128)(2,1)S(1)}, u32[]{:S(2)}, u32[]{:S(2)}) %collective-permute-start.50) | collective-permute-done | bytes 322592 | tf_op jit(solution)/shard_map/ppermute | solution.py:498
  655.2 18.3 %collective-permute-done.52 = bf16[144,1120]{1,0:T(8,128)(2,1)S(1)} collective-permute-done((bf16[144,1120]{1,0:T(8,128)(2,1)S(1)}, bf16[144,1120]{1,0:T(8,128)(2,1)S(1)}, u32[]{:S(2)}, u32[]{:S(2)}) %collective-permute-start.52) | collective-permute-done | bytes 322592 | tf_op jit(solution)/shard_map/ppermute | solution.py:493
  675.1 14.1 %collective-permute-done.53 = bf16[144,1120]{1,0:T(8,128)(2,1)S(1)} collective-permute-done((bf16[144,1120]{1,0:T(8,128)(2,1)S(1)}, bf16[144,1120]{1,0:T(8,128)(2,1)S(1)}, u32[]{:S(2)}, u32[]{:S(2)}) %collective-permute-start.53) | collective-permute-done | bytes 322592 | tf_op jit(solution)/shard_map/ppermute | solution.py:493
  709.8 43.6 %psum.7 = f32[4,3360]{1,0:T(4,128)S(1)} all-reduce(f32[4,3360]{1,0:T(4,128)S(1)} %concatenate.116), channel_id=1, replica_groups=mesh['wide'=8,'narrow'=4] {'wide','narrow'}, use_global_device_ids=true, to_apply=%region_2.3 | all-reduce | flops 13440 | bytes 107520 | tf_op jit(solution)/shard_map/psum | solution.py:688
  (358 shorter events, 259.7 us)
Async XLA Ops:
  11.8 42.0 %collective-permute-start.12 = (bf16[144,1120]{1,0:T(8,128)(2,1)S(1)}, bf16[144,1120]{1,0:T(8,128)(2,1)S(1)}, u32[]{:S(2)}, u32[]{:S(2)}) collective-permute-start(bf16[144,1120]{1,0:T(8,128)(2,1)S(1)} %dynamic-slice_bitcast_fusion.5), channel_id=1, source_target_pairs={{0,1},{1,2},{2,3},{3,0},{4,5},{5,6},{6,7},{7,4},{8,9},{9,10},{10,1... | collective-permute-start | bytes 967688 | tf_op jit(solution)/shard_map/ppermute | solution.py:498
  12.5 59.1 %collective-permute-start.13 = (bf16[144,1120]{1,0:T(8,128)(2,1)S(1)}, bf16[144,1120]{1,0:T(8,128)(2,1)S(1)}, u32[]{:S(2)}, u32[]{:S(2)}) collective-permute-start(bf16[144,1120]{1,0:T(8,128)(2,1)S(1)} %dynamic-slice_bitcast_fusion.5), channel_id=1, source_target_pairs={{0,2},{1,3},{2,0},{3,1},{4,6},{5,7},{6,4},{7,5},{8,10},{9,11},{10,... | collective-permute-start | bytes 967688 | tf_op jit(solution)/shard_map/ppermute | solution.py:498
  15.6 58.8 %collective-permute-start.14 = (bf16[144,1120]{1,0:T(8,128)(2,1)S(1)}, bf16[144,1120]{1,0:T(8,128)(2,1)S(1)}, u32[]{:S(2)}, u32[]{:S(2)}) collective-permute-start(bf16[144,1120]{1,0:T(8,128)(2,1)S(1)} %dynamic-slice_bitcast_fusion.5), channel_id=1, source_target_pairs={{0,3},{1,0},{2,1},{3,2},{4,7},{5,4},{6,5},{7,6},{8,11},{9,8},{10,9... | collective-permute-start | bytes 967688 | tf_op jit(solution)/shard_map/ppermute | solution.py:498
  30.0 60.1 %collective-permute-start.23 = (bf16[3,144,1120]{2,1,0:T(8,128)(2,1)S(1)}, bf16[3,144,1120]{2,1,0:T(8,128)(2,1)S(1)}, u32[]{:S(2)}, u32[]{:S(2)}) collective-permute-start(bf16[3,144,1120]{2,1,0:T(8,128)(2,1)S(1)} %get-tuple-element.188), channel_id=1, source_target_pairs={{0,8},{4,12},{8,0},{12,4},{16,24},{20,28},{24,16},{28,20},{1,9},{5... | collective-permute-start | bytes 2903048 | tf_op jit(solution)/shard_map/ppermute | solution.py:493
  31.8 44.2 %collective-permute-start.1 = (bf16[144,1120]{1,0:T(8,128)(2,1)S(1)}, bf16[144,1120]{1,0:T(8,128)(2,1)S(1)}, u32[]{:S(2)}, u32[]{:S(2)}) collective-permute-start(bf16[144,1120]{1,0:T(8,128)(2,1)S(1)} %dynamic-slice_bitcast_fusion.6), channel_id=1, source_target_pairs={{0,1},{1,2},{2,3},{3,0},{4,5},{5,6},{6,7},{7,4},{8,9},{9,10},{10,1... | collective-permute-start | bytes 967688 | tf_op jit(solution)/shard_map/ppermute | solution.py:498
  90.1 51.8 %collective-permute-start.5 = (bf16[3,144,1120]{2,1,0:T(8,128)(2,1)S(1)}, bf16[3,144,1120]{2,1,0:T(8,128)(2,1)S(1)}, u32[]{:S(2)}, u32[]{:S(2)}) collective-permute-start(bf16[3,144,1120]{2,1,0:T(8,128)(2,1)S(1)} %get-tuple-element.192), channel_id=1, source_target_pairs={{0,16},{4,20},{8,24},{12,28},{16,0},{20,4},{24,8},{28,12},{1,17},{... | collective-permute-start | bytes 2903048 | tf_op jit(solution)/shard_map/ppermute | solution.py:493
  99.3 53.3 %collective-permute-start.25 = (bf16[3,72,1120]{2,1,0:T(8,128)(2,1)S(1)}, bf16[3,72,1120]{2,1,0:T(8,128)(2,1)S(1)}, u32[]{:S(2)}, u32[]{:S(2)}) collective-permute-start(bf16[3,72,1120]{2,1,0:T(8,128)(2,1)S(1)} %slice.457), channel_id=1, source_target_pairs={{0,16},{4,20},{8,24},{12,28},{16,0},{20,4},{24,8},{28,12},{1,17},{... | collective-permute-start | bytes 1451528 | tf_op jit(solution)/shard_map/ppermute | solution.py:493
  101.1 53.1 %collective-permute-start.26 = (bf16[3,72,1120]{2,1,0:T(8,128)(2,1)S(1)}, bf16[3,72,1120]{2,1,0:T(8,128)(2,1)S(1)}, u32[]{:S(2)}, u32[]{:S(2)}) collective-permute-start(bf16[3,72,1120]{2,1,0:T(8,128)(2,1)S(1)} %slice.458), channel_id=1, source_target_pairs={{0,8},{4,12},{8,0},{12,4},{16,24},{20,28},{24,16},{28,20},{1,9},{5... | collective-permute-start | bytes 1451528 | tf_op jit(solution)/shard_map/ppermute | solution.py:493
  120.6 52.2 %collective-permute-start.17 = (bf16[3,72,1120]{2,1,0:T(8,128)(2,1)S(1)}, bf16[3,72,1120]{2,1,0:T(8,128)(2,1)S(1)}, u32[]{:S(2)}, u32[]{:S(2)}) collective-permute-start(bf16[3,72,1120]{2,1,0:T(8,128)(2,1)S(1)} %slice.455), channel_id=1, source_target_pairs={{0,16},{4,20},{8,24},{12,28},{16,0},{20,4},{24,8},{28,12},{1,17},{... | collective-permute-start | bytes 1451528 | tf_op jit(solution)/shard_map/ppermute | solution.py:493
  122.4 50.5 %collective-permute-start.18 = (bf16[3,72,1120]{2,1,0:T(8,128)(2,1)S(1)}, bf16[3,72,1120]{2,1,0:T(8,128)(2,1)S(1)}, u32[]{:S(2)}, u32[]{:S(2)}) collective-permute-start(bf16[3,72,1120]{2,1,0:T(8,128)(2,1)S(1)} %slice.456), channel_id=1, source_target_pairs={{0,8},{4,12},{8,0},{12,4},{16,24},{20,28},{24,16},{28,20},{1,9},{5... | collective-permute-start | bytes 1451528 | tf_op jit(solution)/shard_map/ppermute | solution.py:493
  156.5 129.7 %collective-permute-start.27 = (bf16[4,3,144,1120]{3,2,1,0:T(8,128)(2,1)}, bf16[4,3,144,1120]{3,2,1,0:T(8,128)(2,1)}, u32[]{:S(2)}, u32[]{:S(2)}) collective-permute-start(bf16[4,3,144,1120]{3,2,1,0:T(8,128)(2,1)} %pad_maximum_fusion.6.mine_ref), channel_id=1, source_target_pairs={{0,4},{4,0},{8,12},{12,8},{16,20},{20,16},{24,28},{28,24},{1,5},{5... | collective-permute-start | bytes 11612168 | tf_op jit(solution)/shard_map/ppermute | solution.py:493
  172.8 58.8 %collective-permute-start.8 = (bf16[4,3,144,1120]{3,2,1,0:T(8,128)(2,1)}, bf16[4,3,144,1120]{3,2,1,0:T(8,128)(2,1)}, u32[]{:S(2)}, u32[]{:S(2)}) collective-permute-start(bf16[4,3,144,1120]{3,2,1,0:T(8,128)(2,1)} %pad_maximum_fusion.4.mine_ref), channel_id=1, source_target_pairs={{0,4},{4,0},{8,12},{12,8},{16,20},{20,16},{24,28},{28,24},{1,5},{5... | collective-permute-start | bytes 11612168 | tf_op jit(solution)/shard_map/ppermute | solution.py:493
  175.4 119.5 %collective-permute-start.19 = (bf16[4,3,144,1120]{3,2,1,0:T(8,128)(2,1)}, bf16[4,3,144,1120]{3,2,1,0:T(8,128)(2,1)}, u32[]{:S(2)}, u32[]{:S(2)}) collective-permute-start(bf16[4,3,144,1120]{3,2,1,0:T(8,128)(2,1)} %pad_maximum_fusion.5.mine_ref), channel_id=1, source_target_pairs={{0,4},{4,0},{8,12},{12,8},{16,20},{20,16},{24,28},{28,24},{1,5},{5... | collective-permute-start | bytes 11612168 | tf_op jit(solution)/shard_map/ppermute | solution.py:493
  182.5 47.7 %collective-permute-start = (bf16[512,1120]{0,1:T(8,128)(2,1)S(1)}, bf16[512,1120]{0,1:T(8,128)(2,1)S(1)}, u32[]{:S(2)}, u32[]{:S(2)}) collective-permute-start(bf16[512,1120]{0,1:T(8,128)(2,1)S(1)} %bitcast.231), channel_id=1, source_target_pairs={{0,1},{1,2},{2,3},{4,5},{5,6},{6,7},{8,9},{9,10},{10,11},{12,13},{... | collective-permute-start | bytes 3440648 | tf_op jit(solution)/shard_map/ppermute | solution.py:504
  379.6 74.8 %collective-permute-start.59 = (bf16[4,72,1120]{2,1,0:T(8,128)(2,1)}, bf16[4,72,1120]{2,1,0:T(8,128)(2,1)}, u32[]{:S(2)}, u32[]{:S(2)}) collective-permute-start(bf16[4,72,1120]{2,1,0:T(8,128)(2,1)} %get-tuple-element.175), channel_id=1, source_target_pairs={{0,16},{4,20},{8,24},{12,28},{16,0},{20,4},{24,8},{28,12},{1,17},{... | collective-permute-start | bytes 1935368 | tf_op jit(solution)/shard_map/ppermute | solution.py:493
  387.8 144.4 %collective-permute-start.44 = (bf16[4,512,1120]{1,2,0:T(8,128)(2,1)}, bf16[4,512,1120]{1,2,0:T(8,128)(2,1)}, u32[]{:S(2)}, u32[]{:S(2)}) collective-permute-start(bf16[4,512,1120]{1,2,0:T(8,128)(2,1)} %copy.72), channel_id=1, source_target_pairs={{0,4},{4,0},{8,12},{12,8},{16,20},{20,16},{24,28},{28,24},{1,5},{5... | collective-permute-start | bytes 13762568 | tf_op jit(solution)/shard_map/ppermute | solution.py:493
  450.3 54.5 %collective-permute-start.28 = (bf16[2,512,1120]{1,2,0:T(8,128)(2,1)}, bf16[2,512,1120]{1,2,0:T(8,128)(2,1)}, u32[]{:S(2)}, u32[]{:S(2)}) collective-permute-start(bf16[2,512,1120]{1,2,0:T(8,128)(2,1)} %copy.68), channel_id=1, source_target_pairs={{1,0},{2,1},{3,2},{5,4},{6,5},{7,6},{9,8},{10,9},{11,10},{13,12},{... | collective-permute-start | bytes 6881288 | tf_op jit(solution)/shard_map/ppermute | solution.py:504
  456.9 72.1 %collective-permute-start.60 = (bf16[4,144,1120]{2,1,0:T(8,128)(2,1)}, bf16[4,144,1120]{2,1,0:T(8,128)(2,1)}, u32[]{:S(2)}, u32[]{:S(2)}) collective-permute-start(bf16[4,144,1120]{2,1,0:T(8,128)(2,1)} %pad_maximum_fusion.15), channel_id=1, source_target_pairs={{0,8},{4,12},{8,0},{12,4},{16,24},{20,28},{24,16},{28,20},{1,9},{5... | collective-permute-start | bytes 3870728 | tf_op jit(solution)/shard_map/ppermute | solution.py:493
  470.9 58.1 %collective-permute-start.62 = (bf16[4,144,1120]{2,1,0:T(8,128)(2,1)S(1)}, bf16[4,144,1120]{2,1,0:T(8,128)(2,1)}, u32[]{:S(2)}, u32[]{:S(2)}) collective-permute-start(bf16[4,144,1120]{2,1,0:T(8,128)(2,1)S(1)} %pad_maximum_fusion.16), channel_id=1, source_target_pairs={{0,16},{4,20},{8,24},{12,28},{16,0},{20,4},{24,8},{28,12},{1,17},{... | collective-permute-start | bytes 3870728 | tf_op jit(solution)/shard_map/ppermute | solution.py:493
  474.0 68.6 %collective-permute-start.43 = (bf16[1,576,512]{2,1,0:T(8,128)(2,1)}, bf16[1,576,512]{2,1,0:T(8,128)(2,1)S(1)}, u32[]{:S(2)}, u32[]{:S(2)}) collective-permute-start(bf16[1,576,512]{2,1,0:T(8,128)(2,1)} %bitcast.67), channel_id=1, source_target_pairs={{0,4},{4,0},{8,12},{12,8},{16,20},{20,16},{24,28},{28,24},{1,5},{5... | collective-permute-start | bytes 1769480 | tf_op jit(solution)/shard_map/ppermute | solution.py:493
  529.0 59.6 %collective-permute-start.30 = (bf16[4,512,1120]{1,2,0:T(8,128)(2,1)}, bf16[4,512,1120]{1,2,0:T(8,128)(2,1)}, u32[]{:S(2)}, u32[]{:S(2)}) collective-permute-start(bf16[4,512,1120]{1,2,0:T(8,128)(2,1)} %copy.70), channel_id=1, source_target_pairs={{0,4},{4,0},{8,12},{12,8},{16,20},{20,16},{24,28},{28,24},{1,5},{5... | collective-permute-start | bytes 13762568 | tf_op jit(solution)/shard_map/ppermute | solution.py:493
  560.8 35.9 %collective-permute-start.29 = (bf16[2,576,512]{2,1,0:T(8,128)(2,1)}, bf16[2,576,512]{2,1,0:T(8,128)(2,1)}, u32[]{:S(2)}, u32[]{:S(2)}) collective-permute-start(bf16[2,576,512]{2,1,0:T(8,128)(2,1)} %bitcast.48), channel_id=1, source_target_pairs={{0,4},{4,0},{8,12},{12,8},{16,20},{20,16},{24,28},{28,24},{1,5},{5... | collective-permute-start | bytes 3538952 | tf_op jit(solution)/shard_map/ppermute | solution.py:493
  587.3 66.0 %collective-permute-start.68 = (bf16[72,1120]{1,0:T(8,128)(2,1)S(1)}, bf16[72,1120]{1,0:T(8,128)(2,1)}, u32[]{:S(2)}, u32[]{:S(2)}) collective-permute-start(bf16[72,1120]{1,0:T(8,128)(2,1)S(1)} %slice.515), channel_id=1, source_target_pairs={{0,16},{4,20},{8,24},{12,28},{16,0},{20,4},{24,8},{28,12},{1,17},{... | collective-permute-start | bytes 483848 | tf_op jit(solution)/shard_map/ppermute | solution.py:493
  588.6 65.6 %collective-permute-start.69 = (bf16[72,1120]{1,0:T(8,128)(2,1)}, bf16[72,1120]{1,0:T(8,128)(2,1)}, u32[]{:S(2)}, u32[]{:S(2)}) collective-permute-start(bf16[72,1120]{1,0:T(8,128)(2,1)} %slice.516), channel_id=1, source_target_pairs={{0,8},{4,12},{8,0},{12,4},{16,24},{20,28},{24,16},{28,20},{1,9},{5... | collective-permute-start | bytes 483848 | tf_op jit(solution)/shard_map/ppermute | solution.py:493
  637.6 58.4 %collective-permute-start.32 = (bf16[4,144,1120]{2,1,0:T(8,128)(2,1)S(1)}, bf16[4,144,1120]{2,1,0:T(8,128)(2,1)S(1)}, u32[]{:S(2)}, u32[]{:S(2)}) collective-permute-start(bf16[4,144,1120]{2,1,0:T(8,128)(2,1)S(1)} %pad_maximum_fusion.9), channel_id=1, source_target_pairs={{0,8},{4,12},{8,0},{12,4},{16,24},{20,28},{24,16},{28,20},{1,9},{5... | collective-permute-start | bytes 3870728 | tf_op jit(solution)/shard_map/ppermute | solution.py:493
  650.1 45.9 %collective-permute-start.34 = (bf16[4,144,1120]{2,1,0:T(8,128)(2,1)S(1)}, bf16[4,144,1120]{2,1,0:T(8,128)(2,1)S(1)}, u32[]{:S(2)}, u32[]{:S(2)}) collective-permute-start(bf16[4,144,1120]{2,1,0:T(8,128)(2,1)S(1)} %pad_maximum_fusion.10), channel_id=1, source_target_pairs={{0,16},{4,20},{8,24},{12,28},{16,0},{20,4},{24,8},{28,12},{1,17},{... | collective-permute-start | bytes 3870728 | tf_op jit(solution)/shard_map/ppermute | solution.py:493
  653.4 35.8 %collective-permute-start.53 = (bf16[144,1120]{1,0:T(8,128)(2,1)S(1)}, bf16[144,1120]{1,0:T(8,128)(2,1)S(1)}, u32[]{:S(2)}, u32[]{:S(2)}) collective-permute-start(bf16[144,1120]{1,0:T(8,128)(2,1)S(1)} %fusion.13), channel_id=1, source_target_pairs={{0,16},{4,20},{8,24},{12,28},{16,0},{20,4},{24,8},{28,12},{1,17},{... | collective-permute-start | bytes 967688 | tf_op jit(solution)/shard_map/ppermute | solution.py:493
  692.1 67.0 %collective-permute-start.70 = (bf16[4,144,1120]{2,1,0:T(8,128)(2,1)}, bf16[4,144,1120]{2,1,0:T(8,128)(2,1)S(1)}, u32[]{:S(2)}, u32[]{:S(2)}) collective-permute-start(bf16[4,144,1120]{2,1,0:T(8,128)(2,1)} %pad_maximum_fusion.17), channel_id=1, source_target_pairs={{0,4},{4,0},{8,12},{12,8},{16,20},{20,16},{24,28},{28,24},{1,5},{5... | collective-permute-start | bytes 3870728 | tf_op jit(solution)/shard_map/ppermute | solution.py:493
  696.0 63.1 %collective-permute-start.56 = (bf16[4,144,1120]{2,1,0:T(8,128)(2,1)}, bf16[4,144,1120]{2,1,0:T(8,128)(2,1)}, u32[]{:S(2)}, u32[]{:S(2)}) collective-permute-start(bf16[4,144,1120]{2,1,0:T(8,128)(2,1)} %pad_maximum_fusion.14), channel_id=1, source_target_pairs={{0,4},{4,0},{8,12},{12,8},{16,20},{20,16},{24,28},{28,24},{1,5},{5... | collective-permute-start | bytes 3870728 | tf_op jit(solution)/shard_map/ppermute | solution.py:493
  697.5 57.3 %collective-permute-start.35 = (bf16[144,1120]{1,0:T(8,128)(2,1)}, bf16[144,1120]{1,0:T(8,128)(2,1)}, u32[]{:S(2)}, u32[]{:S(2)}) collective-permute-start(bf16[144,1120]{1,0:T(8,128)(2,1)} %get-tuple-element.182), channel_id=1, source_target_pairs={{0,1},{1,2},{2,3},{3,0},{4,5},{5,6},{6,7},{7,4},{8,9},{9,10},{10,1... | collective-permute-start | bytes 967688 | tf_op jit(solution)/shard_map/ppermute | solution.py:498
  700.1 54.8 %collective-permute-start.36 = (bf16[144,1120]{1,0:T(8,128)(2,1)}, bf16[144,1120]{1,0:T(8,128)(2,1)}, u32[]{:S(2)}, u32[]{:S(2)}) collective-permute-start(bf16[144,1120]{1,0:T(8,128)(2,1)} %get-tuple-element.184), channel_id=1, source_target_pairs={{0,2},{1,3},{2,0},{3,1},{4,6},{5,7},{6,4},{7,5},{8,10},{9,11},{10,... | collective-permute-start | bytes 967688 | tf_op jit(solution)/shard_map/ppermute | solution.py:498
  703.5 51.4 %collective-permute-start.37 = (bf16[144,1120]{1,0:T(8,128)(2,1)}, bf16[144,1120]{1,0:T(8,128)(2,1)}, u32[]{:S(2)}, u32[]{:S(2)}) collective-permute-start(bf16[144,1120]{1,0:T(8,128)(2,1)} %get-tuple-element.183), channel_id=1, source_target_pairs={{0,3},{1,0},{2,1},{3,2},{4,7},{5,4},{6,5},{7,6},{8,11},{9,8},{10,9... | collective-permute-start | bytes 967688 | tf_op jit(solution)/shard_map/ppermute | solution.py:498
  (84 other events, 1201.5 us)

commit v2 on v1

v2 whole, which is shorter than its diff:
```python
import functools

import jax
import jax.numpy as jnp
from jax import lax
from jax.experimental import pallas as pl
from jax.experimental.pallas import tpu as pltpu
from jax.sharding import PartitionSpec as P

HEADS = 20
HEAD = 56
EPS = 1e-05
BF = jnp.bfloat16
F32 = jnp.float32
ROOT_HALF = 0.7071067811865476
INV_ROOT_2PI = 0.3989422804014327
LOG2_E = 1.4426950408889634
VMEM_LIMIT = 60 * 1024 * 1024


def params(n):
    return pltpu.CompilerParams(
        dimension_semantics=("arbitrary",) * n, vmem_limit_bytes=VMEM_LIMIT
    )


def mm(a, b):
    return jnp.dot(a, b, preferred_element_type=F32)


def mm_nt(a, b):
    return lax.dot_general(a, b, (((1,), (1,)), ((), ())), preferred_element_type=F32)


def mm_tn(a, b):
    return lax.dot_general(a, b, (((0,), (0,)), ((), ())), preferred_element_type=F32)


def standardize(values):
    mean = jnp.mean(values, axis=-1, keepdims=True)
    centered = values - mean
    var = jnp.mean(centered * centered, axis=-1, keepdims=True)
    inv = lax.rsqrt(var + EPS)
    return centered * inv, inv


def norm_pullback(grad, normed, inv, gain):
    scaled = grad * gain
    mean_grad = jnp.mean(scaled, axis=-1, keepdims=True)
    mean_proj = jnp.mean(scaled * normed, axis=-1, keepdims=True)
    return inv * (scaled - mean_grad - normed * mean_proj)


def lanes_of(width):
    return -(-width // 128) * 128


def padded(value, width):
    return jnp.concatenate(
        [value, jnp.zeros(value.shape[:-1] + (width - value.shape[-1],), value.dtype)], axis=-1
    )


def head_groups(lanes):
    groups = []
    for h in range(HEADS):
        if groups and (h + 1) * HEAD <= groups[-1][0] + 256:
            groups[-1][1].append(h)
        else:
            groups.append((min(h * HEAD // 128, lanes // 128 - 2) * 128, [h]))
    return groups


def own_lanes(start, h):
    lane = lax.broadcasted_iota(jnp.int32, (1, 256), 1) + start
    return (lane >= h * HEAD) & (lane < (h + 1) * HEAD)


def per_head(value, start, heads):
    wide = value.astype(F32)
    return jnp.concatenate(
        [jnp.where(own_lanes(start, h), wide, 0.0).astype(value.dtype) for h in heads], axis=0
    )


def joined(value, start, heads):
    rows = value.shape[0] // len(heads)
    total = None
    for i, h in enumerate(heads):
        term = jnp.where(own_lanes(start, h), value[i * rows : (i + 1) * rows], 0.0)
        total = term if total is None else total + term
    return total


def by_need(needed, band_blocks, run):
    widths = sorted({min(w, band_blocks) for w in (2, 3, band_blocks)})
    below = 0
    for w in widths:
        pl.when((needed > below) & (needed <= w))(functools.partial(run, w))
        below = w


def qkv_kernel(xp_ref, xo_ref, wq_ref, wk_ref, wv_ref, vec_ref, q_ref, k_ref, v_ref, nt_ref):
    step = pl.program_id(0)
    half = pl.num_programs(0) // 2
    x = jnp.where(step < half, xp_ref[...].astype(F32), xo_ref[...].astype(F32)).T
    normed, _ = standardize(x)
    n = (normed * vec_ref[0:1, :] + vec_ref[1:2, :]).astype(BF)
    lanes = k_ref.shape[1]
    k_ref[...] = padded(mm(n, wk_ref[...]).astype(BF), lanes)
    v_ref[...] = padded((mm(n, wv_ref[...]) + vec_ref[3:4, :]).astype(BF), lanes)

    @pl.when(step >= half)
    def _():
        q_ref[...] = padded((mm(n, wq_ref[...]) + vec_ref[2:3, :]).astype(BF), lanes)
        nt_ref[...] = n.T


def ln_qkv(x_prev, x_own, wa, vec, tb):
    d, t = x_own.shape
    nb = t // tb
    own = lambda i: (jnp.maximum(i - nb, 0), 0)
    weight = lambda s: pl.BlockSpec((None, d, d), lambda i: (s, 0, 0))
    return pl.pallas_call(
        qkv_kernel,
        grid=(2 * nb,),
        in_specs=[
            pl.BlockSpec((d, tb), lambda i: (0, jnp.minimum(i, nb - 1))),
            pl.BlockSpec((d, tb), lambda i: (0, jnp.maximum(i - nb, 0))),
            weight(0),
            weight(1),
            weight(2),
            pl.BlockSpec(vec.shape, lambda i: (0, 0)),
        ],
        out_specs=[
            pl.BlockSpec((tb, lanes_of(d)), own),
            pl.BlockSpec((tb, lanes_of(d)), lambda i: (i, 0)),
            pl.BlockSpec((tb, lanes_of(d)), lambda i: (i, 0)),
            pl.BlockSpec((d, tb), lambda i: (0, jnp.maximum(i - nb, 0))),
        ],
        out_shape=[
            jax.ShapeDtypeStruct((t, lanes_of(d)), BF),
            jax.ShapeDtypeStruct((2 * t, lanes_of(d)), BF),
            jax.ShapeDtypeStruct((2 * t, lanes_of(d)), BF),
            jax.ShapeDtypeStruct((d, t), BF),
        ],
        compiler_params=params(1),
        name="ln_qkv",
    )(x_prev, x_own, wa, wa, wa, vec)


def attend_kernel(need_ref, q_ref, k_ref, v_ref, qid_ref, kid_ref, o_ref, acc_ref):
    step = pl.program_id(0)
    block, lanes = q_ref.shape
    band = kid_ref.shape[-1]
    acc_ref[...] = jnp.zeros_like(acc_ref)

    def run(blocks):
        size = blocks * block
        keys = pl.ds(pl.multiple_of(step * block + band - size, block), size)
        row = lax.broadcasted_iota(jnp.int32, (block, size), 0)
        col = lax.broadcasted_iota(jnp.int32, (block, size), 1)
        allowed = (qid_ref[...] == kid_ref[:, band - size :]) & (col <= row + (size - block))
        bias = jnp.where(allowed, 0.0, -1e30)

        for start, heads in head_groups(lanes):
            window = slice(start, start + 256)
            query = per_head(q_ref[:, window], start, heads)
            scores = mm_nt(query, k_ref[keys, window]) * (HEAD**-0.5 * LOG2_E)
            scores += jnp.concatenate([bias] * len(heads), axis=0)
            e = jnp.exp2(scores - jnp.max(scores, axis=-1, keepdims=True))
            probs = (e * (1.0 / jnp.sum(e, axis=-1, keepdims=True))).astype(BF)
            acc_ref[:, window] += joined(mm(probs, v_ref[keys, window]), start, heads)

    by_need(need_ref[step], band // block, run)
    o_ref[...] = acc_ref[:, : o_ref.shape[1]].astype(BF)


def attend(need, q, k, v, qid, kid, block, d):
    t, lanes = q.shape
    band = kid.shape[-1]
    whole = pl.BlockSpec((2 * t, lanes), lambda i, s: (0, 0))
    return pl.pallas_call(
        attend_kernel,
        grid_spec=pltpu.PrefetchScalarGridSpec(
            num_scalar_prefetch=1,
            grid=(t // block,),
            in_specs=[
                pl.BlockSpec((block, lanes), lambda i, s: (i, 0)),
                whole,
                whole,
                pl.BlockSpec((block, 1), lambda i, s: (i, 0)),
                pl.BlockSpec((None, 1, band), lambda i, s: (i, 0, 0)),
            ],
            out_specs=pl.BlockSpec((block, d), lambda i, s: (i, 0)),
            scratch_shapes=[pltpu.VMEM((block, lanes), F32)],
        ),
        out_shape=jax.ShapeDtypeStruct((t, d), BF),
        compiler_params=params(1),
        name="attend",
    )(need, q, k, v, qid, kid)


def attend_back_kernel(
    need_ref, q_ref, k_ref, v_ref, g_ref, qid_ref, kid_ref,
    dq_ref, prev_ref, own_ref, acc_ref, dk_ref, dv_ref,
):
    step = pl.program_id(0)
    block, lanes = q_ref.shape
    width = dq_ref.shape[1]
    band = kid_ref.shape[0]
    span = dk_ref.shape[0] // 2
    scale = HEAD**-0.5

    @pl.when(step == 0)
    def _():
        dk_ref[...] = jnp.zeros_like(dk_ref)
        dv_ref[...] = jnp.zeros_like(dv_ref)

    acc_ref[...] = jnp.zeros_like(acc_ref)

    def run(blocks):
        size = blocks * block
        keys = pl.ds(pl.multiple_of(step * block + band - size, block), size)
        row = lax.broadcasted_iota(jnp.int32, (size, block), 0)
        col = lax.broadcasted_iota(jnp.int32, (size, block), 1)
        allowed = (qid_ref[...] == kid_ref[band - size :, :]) & (row <= col + (size - block))
        bias = jnp.where(allowed, 0.0, -1e30)

        for start, heads in head_groups(lanes):
            window = slice(start, start + 256)
            query = per_head(q_ref[:, window], start, heads)
            grad = per_head(g_ref[:, window], start, heads)
            key = k_ref[keys, window]
            scores = mm_nt(key, query) * (scale * LOG2_E)
            scores += jnp.concatenate([bias] * len(heads), axis=1)
            e = jnp.exp2(scores - jnp.max(scores, axis=0, keepdims=True))
            probs = e * (1.0 / jnp.sum(e, axis=0, keepdims=True))
            grad_probs = mm_nt(v_ref[keys, window], grad)
            dv_ref[keys, window] += mm(probs.astype(BF), grad)
            dot = jnp.sum(grad_probs * probs, axis=0, keepdims=True)
            grad_scores = (probs * (grad_probs - dot)).astype(BF)
            dk_ref[keys, window] += mm(grad_scores, query)
            acc_ref[:, window] += joined(mm_tn(grad_scores, key), start, heads)

    by_need(need_ref[step], band // block, run)
    dq_ref[...] = (acc_ref[:, :width] * scale).astype(BF)

    @pl.when(step == pl.num_programs(0) - 1)
    def _():
        prev_ref[0] = (dk_ref[0:span, :] * scale).astype(BF)
        prev_ref[1] = dv_ref[0:span, :].astype(BF)
        own_ref[0] = dk_ref[span : 2 * span, :width] * scale
        own_ref[1] = dv_ref[span : 2 * span, :width]


def attend_back(need, q, k, v, grad, qid, kid, block, d):
    t, lanes = q.shape
    band = kid.shape[1]
    whole = pl.BlockSpec((2 * t, lanes), lambda i, s: (0, 0))
    rows = pl.BlockSpec((block, lanes), lambda i, s: (i, 0))
    return pl.pallas_call(
        attend_back_kernel,
        grid_spec=pltpu.PrefetchScalarGridSpec(
            num_scalar_prefetch=1,
            grid=(t // block,),
            in_specs=[
                rows,
                whole,
                whole,
                rows,
                pl.BlockSpec((1, block), lambda i, s: (0, i)),
                pl.BlockSpec((None, band, 1), lambda i, s: (i, 0, 0)),
            ],
            out_specs=[
                pl.BlockSpec((block, d), lambda i, s: (i, 0)),
                pl.BlockSpec((2, t, lanes), lambda i, s: (0, 0, 0)),
                pl.BlockSpec((2, t, d), lambda i, s: (0, 0, 0)),
            ],
            scratch_shapes=[
                pltpu.VMEM((block, lanes), F32),
                pltpu.VMEM((2 * t, lanes), F32),
                pltpu.VMEM((2 * t, lanes), F32),
            ],
        ),
        out_shape=[
            jax.ShapeDtypeStruct((t, d), BF),
            jax.ShapeDtypeStruct((2, t, lanes), BF),
            jax.ShapeDtypeStruct((2, t, d), F32),
        ],
        compiler_params=params(1),
        name="attend_back",
    )(need, q, k, v, grad, qid, kid)


def mlp_kernel(
    x_ref, mixed_ref, cot_ref, wo_ref, wf_ref, wp_ref, vec_ref, bfc_ref,
    out_ref, ht_ref, gp_ref, nt_ref, mt_ref, ga_ref, gb_ref, gm_ref, gbfc_ref, sums_ref,
    after_ref, n_ref, oacc_ref, gacc_ref,
):
    chunk, tok = pl.program_id(0), pl.program_id(1)
    last = pl.num_programs(0) - 1
    tb, width = mixed_ref.shape
    rows = pl.ds(pl.multiple_of(tok * tb, tb), tb)

    @pl.when(chunk == 0)
    def _():
        mixed = mixed_ref[...]
        after = x_ref[...].astype(F32).T + (mm(mixed, wo_ref[...]) + vec_ref[0:1, :])
        normed, _ = standardize(after)
        n = (normed * vec_ref[1:2, :] + vec_ref[2:3, :]).astype(BF)
        after_ref[rows, :] = after
        n_ref[rows, :] = n
        mt_ref[...] = mixed.T
        nt_ref[...] = n.T
        oacc_ref[rows, :] = after + vec_ref[3:4, :]
        gacc_ref[rows, :] = jnp.zeros_like(after)

    @pl.when((chunk == 0) & (tok == 0))
    def _():
        sums_ref[...] = jnp.zeros_like(sums_ref)

    @pl.when(tok == 0)
    def _():
        gbfc_ref[...] = jnp.zeros_like(gbfc_ref)

    pre = mm(n_ref[rows, :], wf_ref[...]) + bfc_ref[...]
    phi = 0.5 + 0.5 * lax.erf(pre * ROOT_HALF)
    hidden = (pre * phi).astype(BF)
    slope = phi + pre * (jnp.exp(-0.5 * pre * pre) * INV_ROOT_2PI)
    cot = cot_ref[...].T
    grad_pre = (mm_nt(cot, wp_ref[...]) * slope).astype(BF)
    oacc_ref[rows, :] += mm(hidden, wp_ref[...])
    gacc_ref[rows, :] += mm_nt(grad_pre, wf_ref[...])
    gp_ref[:, :width] = grad_pre
    ht_ref[...] = hidden.T
    gbfc_ref[...] += jnp.sum(grad_pre.astype(F32), axis=0, keepdims=True)

    @pl.when(chunk == last)
    def _():
        out_ref[...] = oacc_ref[rows, :].astype(BF).T
        normed, inv = standardize(after_ref[rows, :])
        grad_mid = gacc_ref[rows, :]
        wide_cot = cot.astype(F32)
        grad_after = wide_cot + norm_pullback(grad_mid, normed, inv, vec_ref[1:2, :])
        grad_attn = grad_after.astype(BF)
        ga_ref[...] = grad_after
        gb_ref[...] = grad_attn
        gm_ref[...] = padded(mm_nt(grad_attn, wo_ref[...]).astype(BF), gm_ref.shape[1])
        sums_ref[0:1, :] += jnp.sum(grad_mid * normed, axis=0, keepdims=True)
        sums_ref[1:2, :] += jnp.sum(grad_mid, axis=0, keepdims=True)
        sums_ref[2:3, :] += jnp.sum(grad_attn.astype(F32), axis=0, keepdims=True)
        sums_ref[3:4, :] += jnp.sum(wide_cot, axis=0, keepdims=True)


def mlp(x, mixed, cot, wa, wf, wp, vec, bfc, tb):
    d, t = x.shape
    nb, chunks = t // tb, wf.shape[0]
    first = lambda c, i: (jnp.where(c == 0, i, nb - 1), 0)
    first_t = lambda c, i: (0, jnp.where(c == 0, i, nb - 1))
    final = lambda c, i: (jnp.where(c == chunks - 1, i, 0), 0)
    rows = lambda index: pl.BlockSpec((tb, d), index)
    per_chunk = pl.BlockSpec((None, d, d), lambda c, i: (c, 0, 0))
    f32 = jax.ShapeDtypeStruct((t, d), F32)
    bf = jax.ShapeDtypeStruct((t, d), BF)
    bft = jax.ShapeDtypeStruct((d, t), BF)
    return pl.pallas_call(
        mlp_kernel,
        grid=(chunks, nb),
        in_specs=[
            pl.BlockSpec((d, tb), first_t),
            rows(first),
            pl.BlockSpec((d, tb), lambda c, i: (0, i)),
            pl.BlockSpec((None, d, d), lambda c, i: (3, 0, 0)),
            per_chunk,
            per_chunk,
            pl.BlockSpec(vec.shape, lambda c, i: (0, 0)),
            pl.BlockSpec((None, 1, d), lambda c, i: (c, 0, 0)),
        ],
        out_specs=[
            pl.BlockSpec((d, tb), lambda c, i: (0, jnp.where(c == chunks - 1, i, 0))),
            pl.BlockSpec((None, d, tb), lambda c, i: (c, 0, i)),
            pl.BlockSpec((None, tb, lanes_of(d)), lambda c, i: (c, i, 0)),
            pl.BlockSpec((d, tb), first_t),
            pl.BlockSpec((d, tb), first_t),
            rows(final),
            rows(final),
            pl.BlockSpec((tb, lanes_of(d)), final),
            pl.BlockSpec((None, 1, d), lambda c, i: (c, 0, 0)),
            pl.BlockSpec((8, d), lambda c, i: (0, 0)),
        ],
        out_shape=[
            bft,
            jax.ShapeDtypeStruct((chunks, d, t), BF),
            jax.ShapeDtypeStruct((chunks, t, lanes_of(d)), BF),
            bft,
            bft,
            f32,
            bf,
            jax.ShapeDtypeStruct((t, lanes_of(d)), BF),
            jax.ShapeDtypeStruct((chunks, 1, d), F32),
            jax.ShapeDtypeStruct((8, d), F32),
        ],
        scratch_shapes=[
            pltpu.VMEM((t, d), F32),
            pltpu.VMEM((t, d), BF),
            pltpu.VMEM((t, d), F32),
            pltpu.VMEM((t, d), F32),
        ],
        compiler_params=params(2),
        name="mlp",
    )(x, mixed, cot, wa, wf, wp, vec, bfc)


def qkv_back_kernel(
    dq_ref, own_ref, next_ref, gb_ref, x_ref, ga_ref, wq_ref, wk_ref, wv_ref, vec_ref,
    dx_ref, gp_ref, sums_ref,
):
    @pl.when(pl.program_id(0) == 0)
    def _():
        sums_ref[...] = jnp.zeros_like(sums_ref)

    dq = dq_ref[...]
    width = dq.shape[1]
    dk = (own_ref[0] + next_ref[0, :, :width].astype(F32)).astype(BF)
    dv = (own_ref[1] + next_ref[1, :, :width].astype(F32)).astype(BF)
    gp_ref[0, :, :width] = dq
    gp_ref[1, :, :width] = dk
    gp_ref[2, :, :width] = dv
    gp_ref[3, :, :width] = gb_ref[...]
    grad = mm_nt(dq, wq_ref[...]) + mm_nt(dk, wk_ref[...]) + mm_nt(dv, wv_ref[...])
    normed, inv = standardize(x_ref[...].astype(F32).T)
    dx_ref[...] = (ga_ref[...] + norm_pullback(grad, normed, inv, vec_ref[0:1, :])).T
    sums_ref[0:1, :] += jnp.sum(dq.astype(F32), axis=0, keepdims=True)
    sums_ref[1:2, :] += jnp.sum(dv.astype(F32), axis=0, keepdims=True)
    sums_ref[2:3, :] += jnp.sum(grad * normed, axis=0, keepdims=True)
    sums_ref[3:4, :] += jnp.sum(grad, axis=0, keepdims=True)


def qkv_back(dq, own, nxt, gb, x, ga, wa, vec, tb):
    d, t = x.shape
    rows = pl.BlockSpec((tb, d), lambda i: (i, 0))
    turned = pl.BlockSpec((d, tb), lambda i: (0, i))
    pair = pl.BlockSpec((2, tb, d), lambda i: (0, i, 0))
    weight = lambda s: pl.BlockSpec((None, d, d), lambda i: (s, 0, 0))
    return pl.pallas_call(
        qkv_back_kernel,
        grid=(t // tb,),
        in_specs=[
            rows, pair, pl.BlockSpec((2, tb, lanes_of(d)), lambda i: (0, i, 0)), rows, turned, rows,
            weight(0), weight(1), weight(2),
            pl.BlockSpec(vec.shape, lambda i: (0, 0)),
        ],
        out_specs=[
            turned,
            pl.BlockSpec((4, tb, lanes_of(d)), lambda i: (0, i, 0)),
            pl.BlockSpec((8, d), lambda i: (0, 0)),
        ],
        out_shape=[
            jax.ShapeDtypeStruct((d, t), F32),
            jax.ShapeDtypeStruct((4, t, lanes_of(d)), BF),
            jax.ShapeDtypeStruct((8, d), F32),
        ],
        compiler_params=params(1),
        name="qkv_back",
    )(dq, own, nxt, gb, x, ga, wa, wa, wa, vec)


def weight_grad_kernel(turned, groups, extra, count, place_ref, *refs):
    operands, out_refs = refs[:count], refs[count:]
    extra_ref = operands[-1] if extra else None
    size, width = out_refs[0].shape[-2:]
    total = None
    for i in range(0, count - extra, 2):
        if turned:
            term = mm_nt(operands[i][...], operands[i + 1][...])
        else:
            term = mm(operands[i][...], operands[i + 1][:, :width])
        total = term if total is None else total + term
    total = total.astype(BF).reshape(groups, -1, width)
    for r, out_ref in enumerate(out_refs):

        @pl.when(pl.program_id(0) == r)
        def _():
            size = total.shape[1]
            out_ref[:, :size, :] = total
            if extra:
                out_ref[:, size:, :] = extra_ref[...]


def weight_grad(pairs, left_of, right_of, place, d, groups=1, turned=False, extra=None):
    m = pairs[0][0].shape[-2]
    specs, operands = [], []
    for left, right in pairs:
        specs.append(pl.BlockSpec((None,) + left.shape[1:], lambda r, s: (left_of(r, r ^ s[0]), 0, 0)))
        specs.append(pl.BlockSpec((None,) + right.shape[1:], lambda r, s: (right_of(r, r ^ s[0]), 0, 0)))
        operands += [left, right]
    size = m // groups
    if extra is not None:
        specs.append(pl.BlockSpec((None,) + extra.shape[1:], lambda r, s: (r, 0, 0, 0)))
        operands.append(extra)
        size += extra.shape[2]
    return pl.pallas_call(
        functools.partial(
            weight_grad_kernel, turned, groups, extra is not None, len(operands)
        ),
        grid_spec=pltpu.PrefetchScalarGridSpec(
            num_scalar_prefetch=1,
            grid=(4,),
            in_specs=specs,
            out_specs=[pl.BlockSpec((groups, size, d), lambda r, s: (0, 0, 0))] * 4,
        ),
        out_shape=[jax.ShapeDtypeStruct((groups, size, d), BF)] * 4,
        compiler_params=params(1),
        name="weight_grad",
    )(place, *operands)


def assemble_kernel(swapped, place_ref, own_ref, mine_ref, other_ref, out_ref, sems):
    chip, core, depth = place_ref[0], place_ref[1], place_ref[2]
    chunks, block, _ = own_ref.shape
    depths = mine_ref.shape[1] + 1
    piece = mine_ref.shape[2]
    skip = 2 * piece - block

    def target(chunk, z, start, size):
        row = pl.multiple_of((chunk if swapped else z) * block, 8) + start
        return out_ref.at[z if swapped else chunk, pl.ds(pl.multiple_of(row, 8), size), :]

    def run(halves):
        copies = []
        for r in range(chunks):
            chunk = r ^ chip
            copies.append((own_ref.at[chunk], target(chunk, depth, 0, block)))
            for d in range(1, depths):
                z = lax.rem(depth + d, depths)
                copies.append(
                    (halves[0].at[r, d - 1], target(chunk, z, 0, piece))
                )
                copies.append(
                    (
                        halves[1].at[r, d - 1, pl.ds(skip, piece - skip), :],
                        target(chunk, z, piece, piece - skip),
                    )
                )
        started = [
            pltpu.make_async_copy(source, there, sems.at[i])
            for i, (source, there) in enumerate(copies)
        ]
        for copy in started:
            copy.start()
        for copy in started:
            copy.wait()

    @pl.when(core == 0)
    def _():
        run((mine_ref, other_ref))

    @pl.when(core == 1)
    def _():
        run((other_ref, mine_ref))


def assemble(own, mine, other, place, swapped):
    chunks, block, width = own.shape
    depths = mine.shape[1] + 1
    shape = (depths, chunks * block, width) if swapped else (chunks, depths * block, width)
    hbm = pl.BlockSpec(memory_space=pl.ANY)
    return pl.pallas_call(
        functools.partial(assemble_kernel, swapped),
        in_specs=[pl.BlockSpec(memory_space=pltpu.SMEM), hbm, hbm, hbm],
        out_specs=pl.BlockSpec(memory_space=pltpu.VMEM),
        out_shape=jax.ShapeDtypeStruct(shape, own.dtype),
        scratch_shapes=[pltpu.SemaphoreType.DMA((chunks * (2 * depths - 1),))],
        compiler_params=pltpu.CompilerParams(vmem_limit_bytes=VMEM_LIMIT),
        name="assemble",
    )(place, own, mine, other)


def flip(value, bit):
    count = lax.axis_size("wide")
    return lax.ppermute(value, "wide", [(i, i ^ bit) for i in range(count)])


def along(value, distance):
    count = lax.axis_size("narrow")
    return lax.ppermute(value, "narrow", [(i, (i + distance) % count) for i in range(count)])


def from_behind(value, distance):
    count = lax.axis_size("narrow")
    route = [(i - distance, i) for i in range(count) if 0 <= i - distance < count]
    return lax.ppermute(value, "narrow", route)


def add_low(*terms):
    total = terms[0].astype(F32)
    for term in terms[1:]:
        total = total + term.astype(F32)
    return total.astype(BF)


def after(value, *others):
    return lax.optimization_barrier((value, others))[0]


def plane_near(value):
    return flip(value, 2), flip(value, 4)


def plane_far(near):
    across_x, across_y = near
    half = across_x.shape[-2] // 16 * 8
    return flip(across_x[..., :half, :], 4), flip(across_y[..., half:, :], 2)


def plane_all(value, near, far):
    return jnp.stack([value, *near, jnp.concatenate(far, axis=-2)])


def scatter_far(grads):
    half = grads[3].shape[-2] // 16 * 8
    return flip(grads[3][..., :half, :], 2), flip(grads[3][..., half:, :], 4)


def scatter_near(grads, far):
    upper, lower = far
    half = grads[3].shape[-2] // 16 * 8
    to_x = jnp.concatenate(
        [grads[1][..., :half, :], add_low(grads[1][..., half:, :], lower)], axis=-2
    )
    to_y = jnp.concatenate(
        [add_low(grads[2][..., :half, :], upper), grads[2][..., half:, :]], axis=-2
    )
    return to_x, to_y


def depth_scatter(grads):
    parts = [grads[0]]
    for d in range(1, grads.shape[0]):
        parts.append(along(grads[d], d))
    return add_low(*parts)


def roll_from(value, start, axis, count=None):
    count = count or value.shape[axis]
    twice = jnp.concatenate([value, lax.slice_in_dim(value, 0, count, axis=axis)], axis=axis)
    return lax.dynamic_slice_in_dim(twice, start, count, axis=axis)


def shards(
    inputs, cell_lengths, w_qkv, w_out, w_fc, w_proj, b_query, b_value, b_out, b_fc, b_proj,
    gain_attn, shift_attn, gain_mlp, shift_mlp, cotangent,
):
    _, span, d = inputs.shape
    depths = lax.axis_size("narrow")
    chips = lax.axis_size("wide") // 2
    block = w_qkv.shape[0]
    chunks = w_fc.shape[1] // d
    direct = chips == chunks == depths == 4 and block % 8 == 0
    wide_index = lax.axis_index("wide")
    chip, core = wide_index // 2, wide_index % 2
    depth = lax.axis_index("narrow")
    tb = min(256, span)
    qb = 128
    band = span + qb

    x_own = inputs.reshape(span, d).T
    cot = cotangent.reshape(span, d).T

    own_a = jnp.stack([w_qkv[:, i * d : (i + 1) * d] for i in range(3)] + [w_out])
    own_f = jnp.stack([w_fc[:, i * d : (i + 1) * d] for i in range(chunks)])
    small = jnp.concatenate(
        [b_query, b_value, b_out, b_proj, gain_attn, shift_attn, gain_mlp, shift_mlp, b_fc]
    ).reshape(1, -1)
    if direct:
        piece = -(-block // 16) * 8
        place = jnp.stack([chip, core, depth]).astype(jnp.int32)
        own_p = w_proj.reshape(chunks, block, d)

        def part(own):
            return lax.dynamic_slice(own, (chip, core * (block - piece), 0), (1, piece, d))[0]

        small_rows = small.shape[1] // d
        small = jnp.pad(small.reshape(small_rows, d), ((0, 8 - small_rows), (0, 0)))
        part_a = jnp.concatenate([part(own_a), small])
        part_f, part_p = part(own_f), part(own_p)
        arrived = [along(part_a, depths - e) for e in range(1, depths)]
        part_f, part_p = after((part_f, part_p), *arrived)
        x_prev = from_behind(x_own, 1)
        deep_f = lax.all_gather(part_f, "narrow", axis=0)
        deep_p = lax.all_gather(part_p, "narrow", axis=0)
        foreign = after(jnp.stack([a[:piece] for a in arrived]), x_prev)
        near = plane_near(foreign)
        mine = plane_all(foreign, near, plane_far(near))
        mine = after(mine, deep_f)
        other = flip(mine, 1)
        wa = assemble(own_a, mine, other, place, False)
        foreign_f = roll_from(after(deep_f, mine), (depth + 1) % depths, 0, depths - 1)
        near_f = plane_near(foreign_f)
        small = jnp.stack([part_a[piece:]] + [a[piece:] for a in arrived])
        small = roll_from(small, (depths - depth) % depths, 0)[:, :small_rows].reshape(depths, -1)
    else:
        everything = lambda value, axis: lax.all_gather(value, "narrow", axis=axis, tiled=True)
        x_prev = from_behind(x_own, 1)
        wa = everything(own_a, 1)
        wf = everything(own_f, 1)
        wp = everything(w_proj, 0).reshape(chunks, d, d)
        small = everything(small, 0)
    small = small.astype(F32)
    vectors = [small[:, i * block : (i + 1) * block].reshape(1, d) for i in range(8)]
    bias_q, bias_v, bias_o, bias_p, gain_1, shift_1, gain_2, shift_2 = vectors
    bias_f = small[:, 8 * block :].reshape(chunks, 1, d)
    vec_1 = jnp.concatenate([gain_1, shift_1, bias_q, bias_v] + [jnp.zeros_like(bias_q)] * 4)
    vec_2 = jnp.concatenate([bias_o, gain_2, shift_2, bias_p] + [jnp.zeros_like(bias_q)] * 4)

    starts = jnp.cumsum(cell_lengths, axis=-1) - cell_lengths
    pos = (depth - 1) * span + jnp.arange(2 * span, dtype=jnp.int32)
    ids = jnp.sum((starts <= pos[:, None]).astype(jnp.int32), axis=-1) - 1
    query_ids = ids[span:]
    first = ids[span::qb]
    reach = jnp.sum((ids[None, :] < first[:, None]).astype(jnp.int32), axis=-1) // qb
    need = jnp.arange(span // qb, dtype=jnp.int32) + (span // qb + 1) - reach
    key_ids = jnp.stack([ids[i * qb : i * qb + band] for i in range(span // qb)])

    q, k, v, nt_1 = ln_qkv(x_prev, x_own, wa, vec_1, tb)
    if direct:
        near_f, q = after((near_f, q), k)
        far_f = plane_far(near_f)
        foreign_p = roll_from(after(deep_p, *near_f), (depth + 1) % depths, 0, depths - 1)
        near_p = plane_near(foreign_p)
    mixed = attend(need, q, k, v, query_ids[:, None], key_ids[:, None, :], qb, d)
    if direct:
        far_f, near_p = after((far_f, near_p), mixed)
        far_p = plane_far(near_p)
        mine = plane_all(foreign_f, near_f, far_f)
        wf = assemble(own_f, mine, flip(mine, 1), place, False)
        mine = plane_all(foreign_p, near_p, far_p)
        wp = assemble(own_p, mine, flip(mine, 1), place, True)
    out, ht, gp_f, nt_2, mt, grad_after, grad_attn, grad_mixed, grad_bfc, sums_2 = mlp(
        x_own, mixed, cot, wa, wf, wp, vec_2, bias_f, tb
    )
    left_a = jnp.stack([nt_1, mt])
    if direct:
        def halves(value):
            take = lambda at: lax.dynamic_slice_in_dim(value, at * (block - piece), piece, axis=2)
            flat = lambda a: a.reshape(a.shape[0], depths * piece, span)
            return flat(take(core)), flip(flat(take(1 - core)), 1)

        def shard_of(mine, other):
            first = jnp.where(core == 0, mine, other)[:, :piece]
            second = jnp.where(core == 0, other, mine)[:, 2 * piece - block : piece, :]
            both = jnp.concatenate([first, second], axis=1)
            return [
                lax.dynamic_index_in_dim(both, i ^ chip, 0, keepdims=False).astype(F32)
                for i in range(chunks)
            ]

        by_chip = jnp.stack(
            [
                lax.dynamic_index_in_dim(
                    ht.reshape(depths, chunks, block, span), r ^ chip, 1, keepdims=False
                )
                for r in range(chunks)
            ]
        )
        here, there = halves(by_chip)
        cots = cot[None]
        grads_p = weight_grad(
            [(here, cots), (there, flip(cots, 1))],
            lambda r, c: r, lambda r, c: 0, place, d, depths, turned=True,
        )
        here_f, there_f = halves(nt_2.reshape(1, depths, block, span))
        gp_there = flip(gp_f, 1)
        grad_mixed = after(grad_mixed, *grads_p, there_f, gp_there)
        far_p = scatter_far(grads_p)

    dq, kv_prev, kv_own = attend_back(
        need, q, k, v, grad_mixed, query_ids[None, :], key_ids[:, :, None], qb, d
    )
    kv_next = from_behind(kv_prev, -1)
    if direct:
        to_x, to_y = scatter_near(grads_p, after(far_p, kv_prev))
        near_p = (flip(to_x, 2), flip(to_y, 4))
        grads_f = weight_grad(
            [(after(here_f, to_x, to_y), gp_f), (there_f, gp_there)],
            lambda r, c: 0, lambda r, c: c, place, d, depths,
        )
        far_f = scatter_far(grads_f)
        near_p = after(near_p, *grads_f)
        sum_p = add_low(grads_p[0], *near_p)
        to_x, to_y = scatter_near(grads_f, after(far_f, sum_p))
        near_f = (flip(to_x, 2), flip(to_y, 4))
        kv_next = after(kv_next, to_x, to_y)
    dx, gp_a, sums_1 = qkv_back(dq, kv_own, kv_next, grad_attn, x_own, grad_after, wa, vec_1, tb)

    rows = [sums_1[0], sums_1[1], sums_2[2], sums_2[3], sums_1[2], sums_1[3], sums_2[0], sums_2[1]]
    packed = jnp.concatenate(
        [r.reshape(depths, block) for r in rows] + [grad_bfc.reshape(depths, chunks * block)], axis=1
    )
    if direct:
        packed = packed + flip(packed, 1)
        packed = roll_from(packed, depth, 0).reshape(depths, chunks, -1)
        extra = jnp.stack(
            [lax.dynamic_index_in_dim(packed, r ^ chip, 1, keepdims=False) for r in range(chunks)]
        )[:, :, None, :]
        share = extra.shape[-1]
        extra = jnp.pad(extra, ((0, 0), (0, 0), (0, 7), (0, d - share))).astype(BF)
        sum_f = add_low(grads_f[0], *after(near_f, gp_a))
        gp_send = after(gp_a, sum_f)
        sum_p, sum_f = (
            lax.psum_scatter(v, "narrow", scatter_dimension=0, tiled=False) for v in (sum_p, sum_f)
        )
        here, there = halves(roll_from(left_a.reshape(2, depths, block, span), depth, 1))
        grads_a = weight_grad(
            [(here, gp_a), (there, flip(gp_send, 1))],
            lambda r, c: c // 3, lambda r, c: c, place, d, depths, extra=extra,
        )
        to_x, to_y = scatter_near(grads_a, scatter_far(grads_a))
        near_a = after((flip(to_x, 2), flip(to_y, 4)), sum_p, sum_f)
        sum_a = add_low(grads_a[0], *near_a)
        sum_pf = jnp.stack(after((sum_p, sum_f), sum_a))
        near_pf = plane_near(sum_pf)
        far_pf = plane_far(near_pf)
        mine_pf = plane_all(sum_pf, near_pf, far_pf)
        sum_a = after(depth_scatter(sum_a), *far_pf)
        near_a = plane_near(sum_a)
        mine = plane_all(sum_a, near_a, plane_far(near_a))
        other = flip(after(mine, mine_pf), 1)
        other_pf = flip(mine_pf, 1)
        shard_p = shard_of(mine_pf[:, 0], other_pf[:, 0])
        shard_f = shard_of(mine_pf[:, 1], other_pf[:, 1])
        shard_a = shard_of(mine, other)
        shard_p = jnp.concatenate(shard_p, axis=0)
        share_of = mine[:, piece, :share]
        packed = jnp.concatenate(
            [lax.dynamic_index_in_dim(share_of, i ^ chip, 0, keepdims=False) for i in range(chunks)]
        ).astype(F32)
    else:
        zero = jnp.zeros((1,), jnp.int32)

        def total(left, right, left_of, right_of, turned=False):
            grads = weight_grad([(left, right)], left_of, right_of, zero, d, turned=turned)
            return lax.psum(jnp.concatenate(grads).astype(F32), "wide")

        def reduce(grads, axis):
            return lax.psum_scatter(grads, "narrow", scatter_dimension=axis, tiled=True)

        shard_p = total(ht, cot[None], lambda r, c: c, lambda r, c: 0, True)
        shard_p = reduce(shard_p.reshape(chunks * d, d), 0)
        shard_f = reduce(total(nt_2[None], gp_f, lambda r, c: 0, lambda r, c: c), 1)
        shard_a = reduce(total(left_a, gp_a, lambda r, c: c // 3, lambda r, c: c), 1)
        packed = lax.psum(packed, ("wide", "narrow"))
        packed = lax.dynamic_index_in_dim(packed, depth, 0, keepdims=False)
    shard_qkv = jnp.concatenate([shard_a[i] for i in range(3)], axis=1)
    shard_fc = jnp.concatenate([shard_f[i] for i in range(chunks)], axis=1)

    small_grads = [packed[i * block : (i + 1) * block] for i in range(8)]
    g_bq, g_bv, g_bo, g_bp, g_g1, g_s1, g_g2, g_s2 = small_grads
    return (
        out.T.reshape(inputs.shape),
        dx.T.reshape(inputs.shape),
        shard_qkv,
        shard_a[3],
        shard_fc,
        shard_p,
        g_bq,
        g_bv,
        g_bo,
        packed[8 * block :],
        g_bp,
        g_g1,
        g_s1,
        g_g2,
        g_s2,
    )


def solution(mesh):
    rows, flat = P("narrow", None), P("narrow")
    tokens = P("wide", "narrow", None)
    in_specs = (tokens, P("wide", None)) + (rows,) * 4 + (flat,) * 9 + (tokens,)
    out_specs = (tokens, tokens) + (rows,) * 4 + (flat,) * 9
    return jax.shard_map(shards, mesh=mesh, in_specs=in_specs, out_specs=out_specs, check_vma=False)
```

time: 804 us -> 597 us (0.74)
  the two profiles are of different devices: /device:TPU:0 before, /device:TPU:9 now
where the time goes in v2:
time: 597 us; the launch traced here: 586 us
  waiting for transfers between devices  201 us (34%)
  Pallas kernels  187 us (31%)
  starting transfers between devices  63.1 us (11%)
  local copies, waits for them, and re-layouts  62 us (10%)
  other arithmetic  56.7 us (9%)
  between operations  15.4 us (3%)
    ppermute x44, waiting for transfers between devices, flip(): return lax.ppermute(value, 'wide', [(i, i ^ bit) for i in range(count)])  101 us
    ppermute x6, waiting for transfers between devices, along(): lax.ppermute(value, 'narrow', [(i, (i + distance) % count) for i in range...  47.6 us
    ppermute x44, starting transfers between devices, flip(): return lax.ppermute(value, 'wide', [(i, i ^ bit) for i in range(count)])  46.3 us
    pallas_call x1, Pallas kernels, mlp(): pl.pallas_call(mlp_kernel, grid=(chunks, nb), in_specs=[pl.BlockSpec((d,...  43.4 us
    pallas_call x3, Pallas kernels, weight_grad(): pl.pallas_call(functools.partial(weight_grad_kernel, turned, groups, extr...  37.9 us
    ppermute x2, waiting for transfers between devices, from_behind(): return lax.ppermute(value, 'narrow', route)  33.1 us
    pallas_call x1, Pallas kernels, attend_back(): pl.pallas_call(attend_back_kernel, grid_spec=pltpu.PrefetchScalarGridSpec...  31 us
    pallas_call x3, Pallas kernels, assemble(): pl.pallas_call(functools.partial(assemble_kernel, swapped), in_specs=[pl....  26.2 us
  transfers between devices with their start and end apart: 56, of which 28 were waited for; matrix products, arithmetic and copies ran while one was open for 14% of the time, Pallas kernels for 23%

profile of v2, /device:TPU:9, one launch (start us, length us, event | category | flops | bytes accessed | tf_op | source)
XLA Modules:
  0.0 585.5 jit_solution(15052477749183553366)
XLA Ops:
  18.0 24.7 %collective-permute-done.2 = bf16[152,1120]{1,0:T(8,128)(2,1)S(1)} collective-permute-done((bf16[152,1120]{1,0:T(8,128)(2,1)S(1)}, bf16[152,1120]{1,0:T(8,128)(2,1)S(1)}, u32[]{:S(2)}, u32[]{:S(2)}) %collective-permute-start.2) | collective-permute-done | bytes 340512 | tf_op jit(solution)/shard_map/ppermute | solution.py:587
  43.9 23.3 %collective-permute-done.3.xp_ref = bf16[1120,512]{1,0:T(8,128)(2,1)S(1)} collective-permute-done((bf16[1120,512]{1,0:T(8,128)(2,1)S(1)}, bf16[1120,512]{1,0:T(8,128)(2,1)S(1)}, u32[]{:S(2)}, u32[]{:S(2)}) %collective-permute-start.3) | collective-permute-done | bytes 1146912 | tf_op jit(solution)/shard_map/ppermute | solution.py:593
  72.4 17.4 %collective-permute-done.4 = bf16[3,144,1120]{2,1,0:T(8,128)(2,1)} collective-permute-done((bf16[3,144,1120]{2,1,0:T(8,128)(2,1)}, bf16[3,144,1120]{2,1,0:T(8,128)(2,1)}, u32[]{:S(2)}, u32[]{:S(2)}) %collective-permute-start.4) | collective-permute-done | bytes 967712 | tf_op jit(solution)/shard_map/ppermute | solution.py:582
  96.1 5.6 collective-permute-done.6
  106.0 3.6 pad_maximum_fusion.1.mine_ref
  123.3 8.8 %assemble.3.wq_ref.wk_ref.wv_ref.wo_ref = bf16[4,1120,1120]{2,1,0:T(8,128)(2,1)} custom-call(s32[3]{0:T(128)} %pad_add_fusion.1.place_ref, bf16[4,280,1120]{2,1,0:T(8,128)(2,1)} %copy-done.1, bf16[4,3,144,1120]{3,2,1,0:T(8,128)(2,1)} %pad_maximum_fusion.1.mine_ref, bf16[4,3,144,1120]{3,2,1,0:T(8,128)(2,1)} %collective-permute-done.10.other_ref), custom_call_target="tpu_custom_call" | custom-call | tf_op jit(solution)/shard_map/assemble/pallas_call | solution.py:569
  132.2 17.0 %ln_qkv.1 = (bf16[512,1152]{1,0:T(8,128)(2,1)}, bf16[1024,1152]{1,0:T(8,128)(2,1)}, bf16[1024,1152]{1,0:T(8,128)(2,1)}, bf16[1120,512]{1,0:T(8,128)(2,1)}) custom-call(bf16[1120,512]{1,0:T(8,128)(2,1)} %copy-done.30, bf16[1120,512]{1,0:T(8,128)(2,1)} %bitcast.185, bf16[4,1120,1120]{2,1,0:T(8,128)(2,1)} %assemble.3.wq_ref.wk_ref.wv_ref.wo_ref, ...), custom_call_target="tpu_custom_call" | custom-call | tf_op jit(solution)/shard_map/ln_qkv/pallas_call | solution.py:124
  164.5 18.2 %attend.1.mixed_ref = bf16[512,1120]{1,0:T(8,128)(2,1)} custom-call(s32[4]{0:T(128)} %fusion.35.need_ref, bf16[512,1152]{1,0:T(8,128)(2,1)} %get-tuple-element.84.q_ref, bf16[1024,1152]{1,0:T(8,128)(2,1)} %get-tuple-element.83.k_ref, bf16[1024,1152]{1,0:T(8,128)(2,1)} %get-tuple-element.85.v_ref, s32[512,1]{1,0:T(8,128)} %copy.53.qid_ref, ...), custom_call_target="tpu_custom_call" | custom-call | tf_op jit(solution)/shard_map/attend/pallas_call | solution.py:183
  200.2 3.5 pad_maximum_fusion.3.mine_ref
  208.3 8.7 %assemble.4.wf_ref = bf16[4,1120,1120]{2,1,0:T(8,128)(2,1)} custom-call(s32[3]{0:T(128)} %pad_add_fusion.1.place_ref, bf16[4,280,1120]{2,1,0:T(8,128)(2,1)} %copy-done, bf16[4,3,144,1120]{3,2,1,0:T(8,128)(2,1)} %pad_maximum_fusion.2.mine_ref, bf16[4,3,144,1120]{3,2,1,0:T(8,128)(2,1)} %collective-permute-done.15.other_ref), custom_call_target="tpu_custom_call" | custom-call | tf_op jit(solution)/shard_map/assemble/pallas_call | solution.py:569
  217.0 8.7 %assemble.5.wp_ref = bf16[4,1120,1120]{2,1,0:T(8,128)(2,1)} custom-call(s32[3]{0:T(128)} %pad_add_fusion.1.place_ref, bf16[4,280,1120]{2,1,0:T(8,128)(2,1)} %bitcast.202, bf16[4,3,144,1120]{3,2,1,0:T(8,128)(2,1)} %pad_maximum_fusion.3.mine_ref, bf16[4,3,144,1120]{3,2,1,0:T(8,128)(2,1)} %collective-permute-done.18.other_ref), custom_call_target="tpu_custom_call" | custom-call | tf_op jit(solution)/shard_map/assemble/pallas_call | solution.py:569
  225.7 43.4 %mlp.1 = (bf16[1120,512]{1,0:T(8,128)(2,1)}, bf16[4,1120,512]{2,1,0:T(8,128)(2,1)}, bf16[4,512,1152]{2,1,0:T(8,128)(2,1)}, bf16[1120,512]{1,0:T(8,128)(2,1)}, bf...) custom-call(bf16[1120,512]{1,0:T(8,128)(2,1)} %bitcast.186, ...), custom_call_target="tpu_custom_call" | custom-call | tf_op jit(solution)/shard_map/mlp/pallas_call | solution.py:367
  274.8 7.4 %collective-permute-done.20.refs_3_ = bf16[1,1120,512]{2,1,0:T(8,128)(2,1)S(1)} collective-permute-done((bf16[1,1120,512]{2,1,0:T(8,128)(2,1)S(1)}, bf16[1,1120,512]{2,1,0:T(8,128)(2,1)S(1)}, u32[]{:S(2)}, u32[]{:S(2)}) %collective-permute-start.20) | collective-permute-done | bytes 1146912 | tf_op jit(solution)/shard_map/ppermute | solution.py:582
  283.9 12.6 %weight_grad.3 = (bf16[4,144,1120]{2,1,0:T(8,128)(2,1)}, bf16[4,144,1120]{2,1,0:T(8,128)(2,1)}, bf16[4,144,1120]{2,1,0:T(8,128)(2,1)}, bf16[4,144,1120]{2,1,0:T(8,128)(2,1)}) custom-call(s32[3]{0:T(128)} %pad_add_fusion.1.place_ref, bf16[4,576,512]{2,1,0:T(8,128)(2,1)} %bitcast.189, bf16[1,1120,512]{2,1,0:T(8,128)(2,1)} %bitcast.193, ...), custom_call_target="tpu_custom_call" | custom-call | tf_op jit(solution)/shard_map/weight_grad/pallas_call | solution.py:503
  304.3 31.0 %attend_back.1 = (bf16[512,1120]{1,0:T(8,128)(2,1)}, bf16[2,512,1152]{2,1,0:T(8,128)(2,1)}, f32[2,512,1120]{2,1,0:T(8,128)}) custom-call(s32[4]{0:T(128)} %fusion.35.need_ref, bf16[512,1152]{1,0:T(8,128)(2,1)} %get-tuple-element.84.q_ref, bf16[1024,1152]{1,0:T(8,128)(2,1)} %get-tuple-element.83.k_ref, bf16[1024,1152]{1,0:T(8,128)(2,1)} %get-tuple-element.85.v_ref, ...), custom_call_target="tpu_custom_call" | custom-call | tf_op jit(solution)/shard_map/attend_back/pallas_call | solution.py:262
  341.1 12.5 %weight_grad.4 = (bf16[4,144,1120]{2,1,0:T(8,128)(2,1)}, bf16[4,144,1120]{2,1,0:T(8,128)(2,1)}, bf16[4,144,1120]{2,1,0:T(8,128)(2,1)}, bf16[4,144,1120]{2,1,0:T(8,128)(2,1)}) custom-call(s32[3]{0:T(128)} %pad_add_fusion.1.place_ref, bf16[1,576,512]{2,1,0:T(8,128)(2,1)} %bitcast.204, bf16[4,512,1152]{2,1,0:T(8,128)(2,1)} %get-tuple-element.102.refs_1_, ...), custom_call_target="tpu_custom_call" | custom-call | tf_op jit(solution)/shard_map/weight_grad/pallas_call | solution.py:503
  359.2 8.7 %collective-permute-done.29 = bf16[4,144,1120]{2,1,0:T(8,128)(2,1)} collective-permute-done((bf16[4,144,1120]{2,1,0:T(8,128)(2,1)S(1)}, bf16[4,144,1120]{2,1,0:T(8,128)(2,1)}, u32[]{:S(2)}, u32[]{:S(2)}) %collective-permute-start.29) | collective-permute-done | bytes 1290272 | tf_op jit(solution)/shard_map/ppermute | solution.py:582
  374.2 4.5 collective-permute-done.26
  383.0 9.8 %collective-permute-done.23.next_ref = bf16[2,512,1152]{2,1,0:T(8,128)(2,1)} collective-permute-done((bf16[2,512,1152]{2,1,0:T(8,128)(2,1)}, bf16[2,512,1152]{2,1,0:T(8,128)(2,1)}, u32[]{:S(2)}, u32[]{:S(2)}) %collective-permute-start.23) | collective-permute-done | bytes 2359328 | tf_op jit(solution)/shard_map/ppermute | solution.py:593
  392.8 13.8 %qkv_back.1 = (f32[1120,512]{1,0:T(8,128)}, bf16[4,512,1152]{2,1,0:T(8,128)(2,1)}, f32[8,1120]{1,0:T(8,128)}) custom-call(bf16[512,1120]{1,0:T(8,128)(2,1)} %get-tuple-element.104.dq_ref, f32[2,512,1120]{2,1,0:T(8,128)} %get-tuple-element.105.own_ref, bf16[2,512,1152]{2,1,0:T(8,128)(2,1)} %collective-permute-done.23.next_ref, ...), custom_call_target="tpu_custom_call" | custom-call | tf_op jit(solution)/shard_map/qkv_back/pallas_call | solution.py:446
  417.2 4.4 collective-permute-done.34
  423.8 12.9 %weight_grad.5 = (bf16[4,152,1120]{2,1,0:T(8,128)(2,1)}, bf16[4,152,1120]{2,1,0:T(8,128)(2,1)}, bf16[4,152,1120]{2,1,0:T(8,128)(2,1)}, bf16[4,152,1120]{2,1,0:T(8,128)(2,1)}) custom-call(s32[3]{0:T(128)} %pad_add_fusion.1.place_ref, bf16[2,576,512]{2,1,0:T(8,128)(2,1)} %bitcast.190, bf16[4,512,1152]{2,1,0:T(8,128)(2,1)} %get-tuple-element.127.refs_1_, ...), custom_call_target="tpu_custom_call" | custom-call | tf_op jit(solution)/shard_map/weight_grad/pallas_call | solution.py:503
  441.3 13.1 %collective-permute-done.37 = bf16[4,72,1120]{2,1,0:T(8,128)(2,1)} collective-permute-done((bf16[4,72,1120]{2,1,0:T(8,128)(2,1)S(1)}, bf16[4,72,1120]{2,1,0:T(8,128)(2,1)}, u32[]{:S(2)}, u32[]{:S(2)}) %collective-permute-start.37) | collective-permute-done | bytes 645152 | tf_op jit(solution)/shard_map/ppermute | solution.py:582
  461.1 19.3 %reduce-scatter.5.cloned.1.call-done = bf16[1,144,1120]{2,1,0:T(8,128)(2,1)} async-done(((bf16[4,144,1120]{2,1,0:T(8,128)(2,1)}), bf16[1,144,1120]{2,1,0:T(8,128)(2,1)}) %reduce-scatter.5.cloned.1.call-update) | async-done | bytes 322576 | tf_op jit(solution)/shard_map/reduce_scatter | solution.py:812
  480.4 7.7 %collective-permute-done.38 = bf16[4,152,1120]{2,1,0:T(8,128)(2,1)S(1)} collective-permute-done((bf16[4,152,1120]{2,1,0:T(8,128)(2,1)}, bf16[4,152,1120]{2,1,0:T(8,128)(2,1)S(1)}, u32[]{:S(2)}, u32[]{:S(2)}) %collective-permute-start.38) | collective-permute-done | bytes 1361952 | tf_op jit(solution)/shard_map/ppermute | solution.py:582
  495.1 6.9 %collective-permute-start.39 = (bf16[152,1120]{1,0:T(8,128)(2,1)S(1)}, bf16[152,1120]{1,0:T(8,128)(2,1)S(1)}, u32[]{:S(2)}, u32[]{:S(2)}) collective-permute-start(bf16[152,1120]{1,0:T(8,128)(2,1)S(1)} %get-tuple-element.184), channel_id=1, source_target_pairs={{0,1},{1,2},{2,3},{3,0},{4,5},{5,6},{6,7},{7,4},{8,9},{9,10},{10,1... | collective-permute-start | bytes 1021448 | tf_op jit(solution)/shard_map/ppermute | solution.py:587
  503.3 3.5 collective-permute-done.42
  509.5 13.5 %collective-permute-done.39 = bf16[152,1120]{1,0:T(8,128)(2,1)S(1)} collective-permute-done((bf16[152,1120]{1,0:T(8,128)(2,1)S(1)}, bf16[152,1120]{1,0:T(8,128)(2,1)S(1)}, u32[]{:S(2)}, u32[]{:S(2)}) %collective-permute-start.39) | collective-permute-done | bytes 340512 | tf_op jit(solution)/shard_map/ppermute | solution.py:587
  523.0 7.5 %collective-permute-done.40 = bf16[152,1120]{1,0:T(8,128)(2,1)S(1)} collective-permute-done((bf16[152,1120]{1,0:T(8,128)(2,1)S(1)}, bf16[152,1120]{1,0:T(8,128)(2,1)S(1)}, u32[]{:S(2)}, u32[]{:S(2)}) %collective-permute-start.40) | collective-permute-done | bytes 340512 | tf_op jit(solution)/shard_map/ppermute | solution.py:587
  534.9 6.9 %collective-permute-done.47 = bf16[152,1120]{1,0:T(8,128)(2,1)S(1)} collective-permute-done((bf16[152,1120]{1,0:T(8,128)(2,1)S(1)}, bf16[152,1120]{1,0:T(8,128)(2,1)S(1)}, u32[]{:S(2)}, u32[]{:S(2)}) %collective-permute-start.47) | collective-permute-done | bytes 340512 | tf_op jit(solution)/shard_map/ppermute | solution.py:582
  562.2 4.1 select_bitcast_fusion
  568.9 4.1 concatenate.120
  (363 shorter events, 183.2 us)
Async XLA Ops:
  7.2 102.5 %all-gather.5.cloned.1.call-start = ((), (), s32[]{:S(2)}) async-start(), calls=%async_computation.4 | async-start | bytes 1658880 | tf_op jit(solution)/shard_map/all_gather | solution.py:691
  10.4 32.3 %collective-permute-start = (bf16[152,1120]{1,0:T(8,128)(2,1)S(1)}, bf16[152,1120]{1,0:T(8,128)(2,1)S(1)}, u32[]{:S(2)}, u32[]{:S(2)}) collective-permute-start(bf16[152,1120]{1,0:T(8,128)(2,1)S(1)} %pad_maximum_fusion.16), channel_id=1, source_target_pairs={{0,3},{1,0},{2,1},{3,2},{4,7},{5,4},{6,5},{7,6},{8,11},{9,8},{10,9... | collective-permute-start | bytes 1021448 | tf_op jit(solution)/shard_map/ppermute | solution.py:587
  10.5 32.2 %collective-permute-start.1 = (bf16[152,1120]{1,0:T(8,128)(2,1)S(1)}, bf16[152,1120]{1,0:T(8,128)(2,1)S(1)}, u32[]{:S(2)}, u32[]{:S(2)}) collective-permute-start(bf16[152,1120]{1,0:T(8,128)(2,1)S(1)} %pad_maximum_fusion.16), channel_id=1, source_target_pairs={{0,2},{1,3},{2,0},{3,1},{4,6},{5,7},{6,4},{7,5},{8,10},{9,11},{10,... | collective-permute-start | bytes 1021448 | tf_op jit(solution)/shard_map/ppermute | solution.py:587
  13.0 29.7 %collective-permute-start.2 = (bf16[152,1120]{1,0:T(8,128)(2,1)S(1)}, bf16[152,1120]{1,0:T(8,128)(2,1)S(1)}, u32[]{:S(2)}, u32[]{:S(2)}) collective-permute-start(bf16[152,1120]{1,0:T(8,128)(2,1)S(1)} %pad_maximum_fusion.16), channel_id=1, source_target_pairs={{0,1},{1,2},{2,3},{3,0},{4,5},{5,6},{6,7},{7,4},{8,9},{9,10},{10,1... | collective-permute-start | bytes 1021448 | tf_op jit(solution)/shard_map/ppermute | solution.py:587
  15.2 52.1 %collective-permute-start.3 = (bf16[1120,512]{1,0:T(8,128)(2,1)S(1)}, bf16[1120,512]{1,0:T(8,128)(2,1)S(1)}, u32[]{:S(2)}, u32[]{:S(2)}) collective-permute-start(bf16[1120,512]{1,0:T(8,128)(2,1)S(1)} %bitcast.188), channel_id=1, source_target_pairs={{0,1},{1,2},{2,3},{4,5},{5,6},{6,7},{8,9},{9,10},{10,11},{12,13},{... | collective-permute-start | bytes 3440648 | tf_op jit(solution)/shard_map/ppermute | solution.py:593
  67.3 22.5 %collective-permute-start.4 = (bf16[3,144,1120]{2,1,0:T(8,128)(2,1)}, bf16[3,144,1120]{2,1,0:T(8,128)(2,1)}, u32[]{:S(2)}, u32[]{:S(2)}) collective-permute-start(bf16[3,144,1120]{2,1,0:T(8,128)(2,1)} %pad_maximum_fusion.14), channel_id=1, source_target_pairs={{0,8},{4,12},{8,0},{12,4},{16,24},{20,28},{24,16},{28,20},{1,9},{5... | collective-permute-start | bytes 2903048 | tf_op jit(solution)/shard_map/ppermute | solution.py:582
  68.5 23.7 %collective-permute-start.5 = (bf16[3,144,1120]{2,1,0:T(8,128)(2,1)}, bf16[3,144,1120]{2,1,0:T(8,128)(2,1)}, u32[]{:S(2)}, u32[]{:S(2)}) collective-permute-start(bf16[3,144,1120]{2,1,0:T(8,128)(2,1)} %pad_maximum_fusion.14), channel_id=1, source_target_pairs={{0,16},{4,20},{8,24},{12,28},{16,0},{20,4},{24,8},{28,12},{1,17},{... | collective-permute-start | bytes 2903048 | tf_op jit(solution)/shard_map/ppermute | solution.py:582
  72.4 76.8 %all-gather.7.cloned.1.call-start = ((), (), s32[]{:S(2)}) async-start(), calls=%async_computation.5 | async-start | bytes 1658880 | tf_op jit(solution)/shard_map/all_gather | solution.py:692
  113.1 348.0 %reduce-scatter.3.cloned.1.call-start = ((), (), s32[]{:S(2)}) async-start(), calls=%async_computation.2 | async-start | bytes 1658880 | tf_op jit(solution)/shard_map/reduce_scatter | solution.py:812
  117.2 32.0 %collective-permute-start.8 = (bf16[3,144,1120]{2,1,0:T(8,128)(2,1)S(1)}, bf16[3,144,1120]{2,1,0:T(8,128)(2,1)S(1)}, u32[]{:S(2)}, u32[]{:S(2)}) collective-permute-start(bf16[3,144,1120]{2,1,0:T(8,128)(2,1)S(1)} %fusion.1), channel_id=1, source_target_pairs={{0,8},{4,12},{8,0},{12,4},{16,24},{20,28},{24,16},{28,20},{1,9},{5... | collective-permute-start | bytes 2903048 | tf_op jit(solution)/shard_map/ppermute | solution.py:582
  118.4 30.7 %collective-permute-start.9 = (bf16[3,144,1120]{2,1,0:T(8,128)(2,1)S(1)}, bf16[3,144,1120]{2,1,0:T(8,128)(2,1)S(1)}, u32[]{:S(2)}, u32[]{:S(2)}) collective-permute-start(bf16[3,144,1120]{2,1,0:T(8,128)(2,1)S(1)} %fusion.1), channel_id=1, source_target_pairs={{0,16},{4,20},{8,24},{12,28},{16,0},{20,4},{24,8},{28,12},{1,17},{... | collective-permute-start | bytes 2903048 | tf_op jit(solution)/shard_map/ppermute | solution.py:582
  151.9 33.8 %collective-permute-start.13 = (bf16[3,144,1120]{2,1,0:T(8,128)(2,1)S(1)}, bf16[3,144,1120]{2,1,0:T(8,128)(2,1)}, u32[]{:S(2)}, u32[]{:S(2)}) collective-permute-start(bf16[3,144,1120]{2,1,0:T(8,128)(2,1)S(1)} %fusion), channel_id=1, source_target_pairs={{0,8},{4,12},{8,0},{12,4},{16,24},{20,28},{24,16},{28,20},{1,9},{5... | collective-permute-start | bytes 2903048 | tf_op jit(solution)/shard_map/ppermute | solution.py:582
  152.2 33.5 %collective-permute-start.14 = (bf16[3,144,1120]{2,1,0:T(8,128)(2,1)S(1)}, bf16[3,144,1120]{2,1,0:T(8,128)(2,1)}, u32[]{:S(2)}, u32[]{:S(2)}) collective-permute-start(bf16[3,144,1120]{2,1,0:T(8,128)(2,1)S(1)} %fusion), channel_id=1, source_target_pairs={{0,16},{4,20},{8,24},{12,28},{16,0},{20,4},{24,8},{28,12},{1,17},{... | collective-permute-start | bytes 2903048 | tf_op jit(solution)/shard_map/ppermute | solution.py:582
  154.4 31.2 %collective-permute-start.11 = (bf16[3,72,1120]{2,1,0:T(8,128)(2,1)}, bf16[3,72,1120]{2,1,0:T(8,128)(2,1)}, u32[]{:S(2)}, u32[]{:S(2)}) collective-permute-start(bf16[3,72,1120]{2,1,0:T(8,128)(2,1)} %slice.294), channel_id=1, source_target_pairs={{0,16},{4,20},{8,24},{12,28},{16,0},{20,4},{24,8},{28,12},{1,17},{... | collective-permute-start | bytes 1451528 | tf_op jit(solution)/shard_map/ppermute | solution.py:582
  154.7 31.0 %collective-permute-start.12 = (bf16[3,72,1120]{2,1,0:T(8,128)(2,1)S(1)}, bf16[3,72,1120]{2,1,0:T(8,128)(2,1)}, u32[]{:S(2)}, u32[]{:S(2)}) collective-permute-start(bf16[3,72,1120]{2,1,0:T(8,128)(2,1)S(1)} %slice.295), channel_id=1, source_target_pairs={{0,8},{4,12},{8,0},{12,4},{16,24},{20,28},{24,16},{28,20},{1,9},{5... | collective-permute-start | bytes 1451528 | tf_op jit(solution)/shard_map/ppermute | solution.py:582
  269.1 35.1 %collective-permute-start.22 = (bf16[4,512,1152]{2,1,0:T(8,128)(2,1)}, bf16[4,512,1152]{2,1,0:T(8,128)(2,1)}, u32[]{:S(2)}, u32[]{:S(2)}) collective-permute-start(bf16[4,512,1152]{2,1,0:T(8,128)(2,1)} %get-tuple-element.102.refs_1_), channel_id=1, source_target_pairs={{0,4},{4,0},{8,12},{12,8},{16,20},{20,16},{24,28},{28,24},{1,5},{5... | collective-permute-start | bytes 14155784 | tf_op jit(solution)/shard_map/ppermute | solution.py:582
  299.1 36.2 %collective-permute-start.24 = (bf16[4,72,1120]{2,1,0:T(8,128)(2,1)}, bf16[4,72,1120]{2,1,0:T(8,128)(2,1)}, u32[]{:S(2)}, u32[]{:S(2)}) collective-permute-start(bf16[4,72,1120]{2,1,0:T(8,128)(2,1)} %get-tuple-element.190), channel_id=1, source_target_pairs={{0,8},{4,12},{8,0},{12,4},{16,24},{20,28},{24,16},{28,20},{1,9},{5... | collective-permute-start | bytes 1935368 | tf_op jit(solution)/shard_map/ppermute | solution.py:582
  300.2 35.0 %collective-permute-start.25 = (bf16[4,72,1120]{2,1,0:T(8,128)(2,1)}, bf16[4,72,1120]{2,1,0:T(8,128)(2,1)}, u32[]{:S(2)}, u32[]{:S(2)}) collective-permute-start(bf16[4,72,1120]{2,1,0:T(8,128)(2,1)} %get-tuple-element.189), channel_id=1, source_target_pairs={{0,16},{4,20},{8,24},{12,28},{16,0},{20,4},{24,8},{28,12},{1,17},{... | collective-permute-start | bytes 1935368 | tf_op jit(solution)/shard_map/ppermute | solution.py:582
  337.9 30.0 %collective-permute-start.29 = (bf16[4,144,1120]{2,1,0:T(8,128)(2,1)S(1)}, bf16[4,144,1120]{2,1,0:T(8,128)(2,1)}, u32[]{:S(2)}, u32[]{:S(2)}) collective-permute-start(bf16[4,144,1120]{2,1,0:T(8,128)(2,1)S(1)} %pad_maximum_fusion.11), channel_id=1, source_target_pairs={{0,16},{4,20},{8,24},{12,28},{16,0},{20,4},{24,8},{28,12},{1,17},{... | collective-permute-start | bytes 3870728 | tf_op jit(solution)/shard_map/ppermute | solution.py:582
  339.2 31.5 %collective-permute-start.28 = (bf16[4,144,1120]{2,1,0:T(8,128)(2,1)}, bf16[4,144,1120]{2,1,0:T(8,128)(2,1)}, u32[]{:S(2)}, u32[]{:S(2)}) collective-permute-start(bf16[4,144,1120]{2,1,0:T(8,128)(2,1)} %pad_maximum_fusion.10), channel_id=1, source_target_pairs={{0,8},{4,12},{8,0},{12,4},{16,24},{20,28},{24,16},{28,20},{1,9},{5... | collective-permute-start | bytes 3870728 | tf_op jit(solution)/shard_map/ppermute | solution.py:582
  339.2 53.6 %collective-permute-start.23 = (bf16[2,512,1152]{2,1,0:T(8,128)(2,1)}, bf16[2,512,1152]{2,1,0:T(8,128)(2,1)}, u32[]{:S(2)}, u32[]{:S(2)}) collective-permute-start(bf16[2,512,1152]{2,1,0:T(8,128)(2,1)} %get-tuple-element.106), channel_id=1, source_target_pairs={{1,0},{2,1},{3,2},{5,4},{6,5},{7,6},{9,8},{10,9},{11,10},{13,12},{... | collective-permute-start | bytes 7077896 | tf_op jit(solution)/shard_map/ppermute | solution.py:593
  356.2 22.5 %collective-permute-start.26 = (bf16[4,72,1120]{2,1,0:T(8,128)(2,1)}, bf16[4,72,1120]{2,1,0:T(8,128)(2,1)}, u32[]{:S(2)}, u32[]{:S(2)}) collective-permute-start(bf16[4,72,1120]{2,1,0:T(8,128)(2,1)} %get-tuple-element.188), channel_id=1, source_target_pairs={{0,8},{4,12},{8,0},{12,4},{16,24},{20,28},{24,16},{28,20},{1,9},{5... | collective-permute-start | bytes 1935368 | tf_op jit(solution)/shard_map/ppermute | solution.py:582
  380.1 26.5 %collective-permute-start.32 = (bf16[4,144,1120]{2,1,0:T(8,128)(2,1)S(1)}, bf16[4,144,1120]{2,1,0:T(8,128)(2,1)}, u32[]{:S(2)}, u32[]{:S(2)}) collective-permute-start(bf16[4,144,1120]{2,1,0:T(8,128)(2,1)S(1)} %pad_maximum_fusion.13), channel_id=1, source_target_pairs={{0,16},{4,20},{8,24},{12,28},{16,0},{20,4},{24,8},{28,12},{1,17},{... | collective-permute-start | bytes 3870728 | tf_op jit(solution)/shard_map/ppermute | solution.py:582
  382.7 25.8 %collective-permute-start.31 = (bf16[4,144,1120]{2,1,0:T(8,128)(2,1)}, bf16[4,144,1120]{2,1,0:T(8,128)(2,1)}, u32[]{:S(2)}, u32[]{:S(2)}) collective-permute-start(bf16[4,144,1120]{2,1,0:T(8,128)(2,1)} %pad_maximum_fusion.12), channel_id=1, source_target_pairs={{0,8},{4,12},{8,0},{12,4},{16,24},{20,28},{24,16},{28,20},{1,9},{5... | collective-permute-start | bytes 3870728 | tf_op jit(solution)/shard_map/ppermute | solution.py:582
  412.3 68.1 %reduce-scatter.5.cloned.1.call-start = ((), (), s32[]{:S(2)}) async-start(), calls=%async_computation.3 | async-start | bytes 1658880 | tf_op jit(solution)/shard_map/reduce_scatter | solution.py:812
  456.8 31.3 %collective-permute-start.38 = (bf16[4,152,1120]{2,1,0:T(8,128)(2,1)}, bf16[4,152,1120]{2,1,0:T(8,128)(2,1)S(1)}, u32[]{:S(2)}, u32[]{:S(2)}) collective-permute-start(bf16[4,152,1120]{2,1,0:T(8,128)(2,1)} %pad_maximum_fusion.8), channel_id=1, source_target_pairs={{0,16},{4,20},{8,24},{12,28},{16,0},{20,4},{24,8},{28,12},{1,17},{... | collective-permute-start | bytes 4085768 | tf_op jit(solution)/shard_map/ppermute | solution.py:582
  459.6 31.0 %collective-permute-start.36 = (bf16[4,152,1120]{2,1,0:T(8,128)(2,1)}, bf16[4,152,1120]{2,1,0:T(8,128)(2,1)}, u32[]{:S(2)}, u32[]{:S(2)}) collective-permute-start(bf16[4,152,1120]{2,1,0:T(8,128)(2,1)} %pad_maximum_fusion.7), channel_id=1, source_target_pairs={{0,8},{4,12},{8,0},{12,4},{16,24},{20,28},{24,16},{28,20},{1,9},{5... | collective-permute-start | bytes 4085768 | tf_op jit(solution)/shard_map/ppermute | solution.py:582
  495.1 27.9 %collective-permute-start.39 = (bf16[152,1120]{1,0:T(8,128)(2,1)S(1)}, bf16[152,1120]{1,0:T(8,128)(2,1)S(1)}, u32[]{:S(2)}, u32[]{:S(2)}) collective-permute-start(bf16[152,1120]{1,0:T(8,128)(2,1)S(1)} %get-tuple-element.184), channel_id=1, source_target_pairs={{0,1},{1,2},{2,3},{3,0},{4,5},{5,6},{6,7},{7,4},{8,9},{9,10},{10,1... | collective-permute-start | bytes 1021448 | tf_op jit(solution)/shard_map/ppermute | solution.py:587
  502.0 28.5 %collective-permute-start.40 = (bf16[152,1120]{1,0:T(8,128)(2,1)S(1)}, bf16[152,1120]{1,0:T(8,128)(2,1)S(1)}, u32[]{:S(2)}, u32[]{:S(2)}) collective-permute-start(bf16[152,1120]{1,0:T(8,128)(2,1)S(1)} %get-tuple-element.186), channel_id=1, source_target_pairs={{0,2},{1,3},{2,0},{3,1},{4,6},{5,7},{6,4},{7,5},{8,10},{9,11},{10,... | collective-permute-start | bytes 1021448 | tf_op jit(solution)/shard_map/ppermute | solution.py:587
  502.0 30.4 %collective-permute-start.41 = (bf16[152,1120]{1,0:T(8,128)(2,1)S(1)}, bf16[152,1120]{1,0:T(8,128)(2,1)S(1)}, u32[]{:S(2)}, u32[]{:S(2)}) collective-permute-start(bf16[152,1120]{1,0:T(8,128)(2,1)S(1)} %get-tuple-element.185), channel_id=1, source_target_pairs={{0,3},{1,0},{2,1},{3,2},{4,7},{5,4},{6,5},{7,6},{8,11},{9,8},{10,9... | collective-permute-start | bytes 1021448 | tf_op jit(solution)/shard_map/ppermute | solution.py:587
  506.8 25.8 %collective-permute-start.43 = (bf16[2,72,1120]{2,1,0:T(8,128)(2,1)S(1)}, bf16[2,72,1120]{2,1,0:T(8,128)(2,1)S(1)}, u32[]{:S(2)}, u32[]{:S(2)}) collective-permute-start(bf16[2,72,1120]{2,1,0:T(8,128)(2,1)S(1)} %slice.377), channel_id=1, source_target_pairs={{0,16},{4,20},{8,24},{12,28},{16,0},{20,4},{24,8},{28,12},{1,17},{... | collective-permute-start | bytes 967688 | tf_op jit(solution)/shard_map/ppermute | solution.py:582
  508.0 24.6 %collective-permute-start.45 = (bf16[2,72,1120]{2,1,0:T(8,128)(2,1)S(1)}, bf16[2,72,1120]{2,1,0:T(8,128)(2,1)S(1)}, u32[]{:S(2)}, u32[]{:S(2)}) collective-permute-start(bf16[2,72,1120]{2,1,0:T(8,128)(2,1)S(1)} %slice.378), channel_id=1, source_target_pairs={{0,8},{4,12},{8,0},{12,4},{16,24},{20,28},{24,16},{28,20},{1,9},{5... | collective-permute-start | bytes 967688 | tf_op jit(solution)/shard_map/ppermute | solution.py:582
  (80 other events, 564.8 us)
Sparse Core Ops, SparseCore 0:
  72.5 32.3 all-gather.4
  113.2 31.5 all-gather.6
  412.5 35.2 reduce-scatter.2
  449.9 30.4 reduce-scatter.4
